TPU v7x, 32 devices: a whole 2x2x4 slice. The times are simulated.
32 devices in a mesh: dp: 8 (over z, y), tensor: 4 (over x, core).
Axes of the slice: x: 2, y: 2, z: 4, core: 2. Of those that a mesh axis runs over, the one named last changes fastest.
Arguments:
- states: bfloat16 [8192, 1536], P(('dp', 'tensor')), may hold values from -6 to 6
- cotangent: bfloat16 [8192, 1536], P(('dp', 'tensor')), may hold values from -6 to 6
- teacher: bfloat16 [8192, 1536], P(('dp', 'tensor')), may hold values from -9 to 9
- prefix_len: int32 [8], P('dp'), may hold values from 102 to 512
- validity: int32 [8, 1024], P('dp'), may hold values from 0 to 1, as said below
- w_query: bfloat16 [1536, 1536], P('dp', 'tensor'), may hold values from -0.15625 to 0.15625
- key_projection_weight: bfloat16 [1536, 256], P(('dp', 'tensor')), may hold values from -0.15625 to 0.15625
- value_projection_weight: bfloat16 [1536, 256], P(('dp', 'tensor')), may hold values from -0.15625 to 0.15625
- w_output: bfloat16 [1536, 1536], P('tensor', 'dp'), may hold values from -2.5 to 2.5
- w_gate: bfloat16 [1536, 8960], P('dp', 'tensor'), may hold values from -0.15625 to 0.15625
- w_up: bfloat16 [1536, 8960], P('dp', 'tensor'), may hold values from -0.15625 to 0.15625
- w_down: bfloat16 [8960, 1536], P('tensor', 'dp'), may hold values from -0.0625 to 0.0625
- b_query: bfloat16 [1536], P(('dp', 'tensor')), may hold values from -3 to 3
- key_offset_bias: bfloat16 [256], P(('dp', 'tensor')), may hold values from -3 to 3
- value_offset_bias: bfloat16 [256], P(('dp', 'tensor')), may hold values from -0.059814453 to 0.059814453
- gain_attn: bfloat16 [1536], P(('dp', 'tensor')), may hold values from 0.5 to 1.5
- gain_ffn: bfloat16 [1536], P(('dp', 'tensor')), may hold values from 0.5 to 1.5
Outputs:
- layer_out: bfloat16 [8192, 1536], P(('dp', 'tensor'))
- distill_loss: float32 [], replicated
- grad_states: float32 [8192, 1536], P(('dp', 'tensor'))
- grad_w_query: float32 [1536, 1536], P('dp', 'tensor')
- grad_w_key: float32 [1536, 256], P(('dp', 'tensor'))
- grad_w_value: float32 [1536, 256], P(('dp', 'tensor'))
- grad_w_output: float32 [1536, 1536], P('tensor', 'dp')
- grad_w_gate: float32 [1536, 8960], P('dp', 'tensor')
- grad_w_up: float32 [1536, 8960], P('dp', 'tensor')
- grad_w_down: float32 [8960, 1536], P('tensor', 'dp')
- grad_b_query: float32 [1536], P(('dp', 'tensor'))
- grad_b_key: float32 [256], P(('dp', 'tensor'))
- grad_b_value: float32 [256], P(('dp', 'tensor'))
- grad_gain_attn: float32 [1536], P(('dp', 'tensor'))
- grad_gain_ffn: float32 [1536], P(('dp', 'tensor'))
Inputs may be any that keep to these rules, and one draw needn't show every extreme that they name: `validity`: the first token of every sequence is real.
All inputs are finite; a program needn't handle non-finite values.
Results may differ from a plain program's by a relative error of at most 0.017.
Values may be sent and summed in bfloat16 or wider, within the bound.
No kernel may reach another device: no remote copies, remote signals or barrier semaphores. Data moves between devices by JAX's collectives and lax.ppermute only.
A program may use at most 192 MiB of HBM per device.

v0:
```python
import jax
import jax.numpy as jnp
from jax import lax
from jax.sharding import PartitionSpec as P

QUERY_HEADS = 12
KEY_VALUE_HEADS = 2
HEAD_SIZE = 128


NORM_EPS = 1e-06
ROPE_BASE = 10000.0
NEG_FILL = -1e30


def tables(sequence_length, head_width):
    half_width = head_width // 2
    inverse = ROPE_BASE ** (-(jnp.arange(half_width, dtype=jnp.float32) * 2.0 / head_width))
    angles = jnp.arange(sequence_length, dtype=jnp.float32)[:, None] * inverse[None, :]
    return (jnp.cos(angles), jnp.sin(angles))


def rotate(values, cosine, sine):
    half_width = values.shape[-1] // 2
    first = values[..., :half_width]
    second = values[..., half_width:]
    return jnp.concatenate(
        [first * cosine - second * sine, second * cosine + first * sine], axis=-1
    )


def norm_rows(values, gain):
    return values * lax.rsqrt(jnp.mean(values * values, -1, keepdims=True) + NORM_EPS) * gain


def allowed_keys(query_pos, sequence_length, prefix, valid):
    key_pos = jnp.arange(sequence_length, dtype=jnp.int32)
    causal = key_pos[None, :] <= query_pos[:, None]
    return (causal | (key_pos[None, :] < prefix)) & (valid[None, :] > 0)


def body(
    states,
    cotangent,
    teacher,
    prefix_len,
    validity,
    w_query,
    key_projection_weight,
    value_projection_weight,
    w_output,
    w_gate,
    w_up,
    w_down,
    b_query,
    key_offset_bias,
    value_offset_bias,
    gain_attn,
    gain_ffn,
):
    groups = lax.axis_size("tensor")
    tensor_split_index = lax.axis_index("tensor")
    row_count = states.shape[0]
    feature_count = states.shape[1]
    seq_here = prefix_len.shape[0]
    sequence_length = validity.shape[1]
    block_rows = min(512, sequence_length)
    block_count = sequence_length // block_rows
    local_heads = QUERY_HEADS // groups
    head_cols = local_heads * HEAD_SIZE
    all_rows = row_count * groups
    score_scale = HEAD_SIZE ** (-0.5)
    key_value_head = tensor_split_index * local_heads // (QUERY_HEADS // KEY_VALUE_HEADS)
    key_full, value_full, bias_query, bias_key, bias_value, gain_one, gain_two = (
        lax.all_gather(key_projection_weight, ("dp", "tensor"), axis=0, tiled=True),
        lax.all_gather(value_projection_weight, ("dp", "tensor"), axis=0, tiled=True),
        lax.all_gather(b_query, ("dp", "tensor"), axis=0, tiled=True),
        lax.all_gather(key_offset_bias, ("dp", "tensor"), axis=0, tiled=True),
        lax.all_gather(value_offset_bias, ("dp", "tensor"), axis=0, tiled=True),
        lax.all_gather(gain_attn, ("dp", "tensor"), axis=0, tiled=True),
        lax.all_gather(gain_ffn, ("dp", "tensor"), axis=0, tiled=True),
    )
    query_w, output_w, gate_w, up_w, down_w = (
        lax.all_gather(w_query, "dp", axis=0, tiled=True),
        lax.all_gather(w_output, "dp", axis=1, tiled=True),
        lax.all_gather(w_gate, "dp", axis=0, tiled=True),
        lax.all_gather(w_up, "dp", axis=0, tiled=True),
        lax.all_gather(w_down, "dp", axis=1, tiled=True),
    )
    key_w = lax.dynamic_slice_in_dim(key_full, key_value_head * HEAD_SIZE, HEAD_SIZE, 1)
    value_w = lax.dynamic_slice_in_dim(value_full, key_value_head * HEAD_SIZE, HEAD_SIZE, 1)
    query_bias = lax.dynamic_slice_in_dim(
        bias_query, tensor_split_index * head_cols, head_cols, 0
    ).astype(jnp.float32)
    key_bias = lax.dynamic_slice_in_dim(bias_key, key_value_head * HEAD_SIZE, HEAD_SIZE, 0).astype(
        jnp.float32
    )
    value_bias = lax.dynamic_slice_in_dim(
        bias_value, key_value_head * HEAD_SIZE, HEAD_SIZE, 0
    ).astype(jnp.float32)
    gain_first = gain_one.astype(jnp.float32)
    gain_second = gain_two.astype(jnp.float32)
    cosine, sine = tables(sequence_length, HEAD_SIZE)
    states_f = states.astype(jnp.float32)
    normalized_rows = norm_rows(states_f, gain_first).astype(jnp.bfloat16)
    normed_all = lax.all_gather(normalized_rows, "tensor", axis=0, tiled=True)
    query_raw = jnp.dot(normed_all, query_w, preferred_element_type=jnp.float32) + query_bias
    key_raw = jnp.dot(normed_all, key_w, preferred_element_type=jnp.float32) + key_bias
    value_seq = (
        (jnp.dot(normed_all, value_w, preferred_element_type=jnp.float32) + value_bias)
        .astype(jnp.bfloat16)
        .reshape(seq_here, sequence_length, HEAD_SIZE)
    )
    query_seq = rotate(
        query_raw.reshape(seq_here, sequence_length, local_heads, HEAD_SIZE),
        cosine[:, None, :],
        sine[:, None, :],
    ).astype(jnp.bfloat16)
    key_seq = rotate(key_raw.reshape(seq_here, sequence_length, HEAD_SIZE), cosine, sine).astype(
        jnp.bfloat16
    )

    def block_scores(query_blk, key_rows, blk_index, prefix, valid):
        positions = blk_index * block_rows + jnp.arange(block_rows, dtype=jnp.int32)
        scores = (
            jnp.einsum("qhd,kd->hqk", query_blk, key_rows, preferred_element_type=jnp.float32)
            * score_scale
        )
        return jnp.where(
            allowed_keys(positions, sequence_length, prefix, valid)[None], scores, NEG_FILL
        )

    def attend_sequence(inputs):
        queries, key_rows, value_rows, prefix, valid = inputs

        def attend_one_block(carry, blk_index):
            query_blk = lax.dynamic_slice_in_dim(queries, blk_index * block_rows, block_rows, 0)
            scores = block_scores(query_blk, key_rows, blk_index, prefix, valid)
            row_max = jnp.max(scores, -1, keepdims=True)
            shifted = jnp.exp(scores - row_max)
            row_sum = jnp.sum(shifted, -1, keepdims=True)
            probs_low = (shifted / row_sum).astype(jnp.bfloat16)
            mixed = jnp.einsum(
                "hqk,kd->qhd", probs_low, value_rows, preferred_element_type=jnp.float32
            )
            return (carry, (mixed.astype(jnp.bfloat16), row_max, row_sum))

        _, (mixed, row_max, row_sum) = lax.scan(
            attend_one_block, jnp.zeros((), jnp.int32), jnp.arange(block_count, dtype=jnp.int32)
        )
        return (mixed.reshape(sequence_length, head_cols), row_max, row_sum)

    attended, max_saved, sum_saved = lax.map(
        attend_sequence, (query_seq, key_seq, value_seq, prefix_len, validity)
    )
    attended = attended.reshape(all_rows, head_cols)
    branch_attn = lax.psum_scatter(
        jnp.dot(attended, output_w, preferred_element_type=jnp.float32).astype(jnp.bfloat16),
        "tensor",
        scatter_dimension=0,
        tiled=True,
    ).astype(jnp.float32)
    middle = states_f + branch_attn
    normed_two = norm_rows(middle, gain_second).astype(jnp.bfloat16)
    normed_two_all = lax.all_gather(normed_two, "tensor", axis=0, tiled=True)
    gate_act = jnp.dot(normed_two_all, gate_w, preferred_element_type=jnp.float32)
    up_act = jnp.dot(normed_two_all, up_w, preferred_element_type=jnp.float32)
    sigma = jax.nn.sigmoid(gate_act)
    hidden = (gate_act * sigma * up_act).astype(jnp.bfloat16)
    branch_ffn = lax.psum_scatter(
        jnp.dot(hidden, down_w, preferred_element_type=jnp.float32).astype(jnp.bfloat16),
        "tensor",
        scatter_dimension=0,
        tiled=True,
    ).astype(jnp.float32)
    result = middle + branch_ffn
    valid_rows = lax.dynamic_slice_in_dim(
        validity.reshape(-1), tensor_split_index * row_count, row_count, 0
    ).astype(jnp.float32)[:, None]
    deviation = result - teacher.astype(jnp.float32)
    square_sum, count_all = lax.psum(
        (jnp.sum(valid_rows * deviation * deviation), jnp.sum(valid_rows)), ("dp", "tensor")
    )
    token_total = float(all_rows * lax.axis_size("dp"))
    distill_loss = square_sum / (2.0 * count_all * feature_count)
    grad_result = cotangent.astype(jnp.float32) + token_total / count_all * valid_rows * deviation
    query_w, output_w, gate_w, up_w, down_w = (
        lax.all_gather(w_query, "dp", axis=0, tiled=True),
        lax.all_gather(w_output, "dp", axis=1, tiled=True),
        lax.all_gather(w_gate, "dp", axis=0, tiled=True),
        lax.all_gather(w_up, "dp", axis=0, tiled=True),
        lax.all_gather(w_down, "dp", axis=1, tiled=True),
    )
    grad_two_all = lax.all_gather(grad_result.astype(jnp.bfloat16), "tensor", axis=0, tiled=True)
    grad_hidden = jnp.einsum("rd,fd->rf", grad_two_all, down_w, preferred_element_type=jnp.float32)
    grad_down = jnp.einsum("rf,rd->fd", hidden, grad_two_all, preferred_element_type=jnp.float32)
    grad_gate_act = (grad_hidden * up_act * sigma * (1.0 + gate_act * (1.0 - sigma))).astype(
        jnp.bfloat16
    )
    grad_up_act = (grad_hidden * gate_act * sigma).astype(jnp.bfloat16)
    grad_gate = jnp.einsum(
        "rd,rf->df", normed_two_all, grad_gate_act, preferred_element_type=jnp.float32
    )
    grad_up = jnp.einsum(
        "rd,rf->df", normed_two_all, grad_up_act, preferred_element_type=jnp.float32
    )
    grad_normed_two = jnp.einsum(
        "rf,df->rd", grad_gate_act, gate_w, preferred_element_type=jnp.float32
    ) + jnp.einsum("rf,df->rd", grad_up_act, up_w, preferred_element_type=jnp.float32)
    grad_normed_two = lax.psum_scatter(
        grad_normed_two.astype(jnp.bfloat16), "tensor", scatter_dimension=0, tiled=True
    ).astype(jnp.float32)
    _, pull_second = jax.vjp(norm_rows, middle, gain_second)
    grad_mid_norm, grad_gain_second = pull_second(grad_normed_two)
    grad_middle = grad_result + grad_mid_norm
    grad_one_all = lax.all_gather(grad_middle.astype(jnp.bfloat16), "tensor", axis=0, tiled=True)
    grad_output = jnp.einsum(
        "rh,rd->hd", attended, grad_one_all, preferred_element_type=jnp.float32
    )
    grad_attended = (
        jnp.einsum("rd,hd->rh", grad_one_all, output_w, preferred_element_type=jnp.float32)
        .astype(jnp.bfloat16)
        .reshape(seq_here, sequence_length, local_heads, HEAD_SIZE)
    )

    def back_sequence(inputs):
        queries, key_rows, value_rows, grad_mixed, prefix, valid, max_rows, sum_rows = inputs

        def back_one_block(carry, blk_index):
            key_acc, value_acc = carry
            query_blk = lax.dynamic_slice_in_dim(queries, blk_index * block_rows, block_rows, 0)
            grad_blk = lax.dynamic_slice_in_dim(grad_mixed, blk_index * block_rows, block_rows, 0)
            scores = block_scores(query_blk, key_rows, blk_index, prefix, valid)
            probs = jnp.exp(scores - max_rows[blk_index]) / sum_rows[blk_index]
            grad_probs = jnp.einsum(
                "qhd,kd->hqk", grad_blk, value_rows, preferred_element_type=jnp.float32
            )
            spread = jnp.sum(probs * grad_probs, -1, keepdims=True)
            grad_scores = (probs * (grad_probs - spread)).astype(jnp.bfloat16)
            grad_query = (
                jnp.einsum("hqk,kd->qhd", grad_scores, key_rows, preferred_element_type=jnp.float32)
                * score_scale
            )
            key_acc = (
                key_acc
                + jnp.einsum(
                    "hqk,qhd->kd", grad_scores, query_blk, preferred_element_type=jnp.float32
                )
                * score_scale
            )
            value_acc = value_acc + jnp.einsum(
                "hqk,qhd->kd",
                probs.astype(jnp.bfloat16),
                grad_blk,
                preferred_element_type=jnp.float32,
            )
            return ((key_acc, value_acc), grad_query)

        zero_rows = jnp.zeros((sequence_length, HEAD_SIZE), jnp.float32)
        (key_acc, value_acc), grad_query = lax.scan(
            back_one_block, (zero_rows, zero_rows), jnp.arange(block_count, dtype=jnp.int32)
        )
        return (grad_query.reshape(sequence_length, local_heads, HEAD_SIZE), key_acc, value_acc)

    grad_query_seq, grad_key_seq, grad_value_seq = lax.map(
        back_sequence,
        (query_seq, key_seq, value_seq, grad_attended, prefix_len, validity, max_saved, sum_saved),
    )
    grad_query_raw = (
        rotate(grad_query_seq, cosine[:, None, :], -sine[:, None, :])
        .astype(jnp.bfloat16)
        .reshape(all_rows, head_cols)
    )
    grad_key_raw = (
        rotate(grad_key_seq, cosine, -sine).astype(jnp.bfloat16).reshape(all_rows, HEAD_SIZE)
    )
    grad_value_raw = grad_value_seq.astype(jnp.bfloat16).reshape(all_rows, HEAD_SIZE)
    grad_query = jnp.einsum(
        "rd,rh->dh", normed_all, grad_query_raw, preferred_element_type=jnp.float32
    )
    grad_key = jnp.einsum("rd,rk->dk", normed_all, grad_key_raw, preferred_element_type=jnp.float32)
    grad_value = jnp.einsum(
        "rd,rk->dk", normed_all, grad_value_raw, preferred_element_type=jnp.float32
    )
    grad_query_bias = jnp.sum(grad_query_raw.astype(jnp.float32), 0)
    grad_key_bias = jnp.sum(grad_key_raw.astype(jnp.float32), 0)
    grad_value_bias = jnp.sum(grad_value_raw.astype(jnp.float32), 0)
    grad_normed = jnp.einsum(
        "rh,dh->rd", grad_query_raw, query_w, preferred_element_type=jnp.float32
    )
    grad_normed = grad_normed + jnp.einsum(
        "rk,dk->rd", grad_key_raw, key_w, preferred_element_type=jnp.float32
    )
    grad_normed = grad_normed + jnp.einsum(
        "rk,dk->rd", grad_value_raw, value_w, preferred_element_type=jnp.float32
    )
    grad_normed = lax.psum_scatter(
        grad_normed.astype(jnp.bfloat16), "tensor", scatter_dimension=0, tiled=True
    ).astype(jnp.float32)
    _, pull_first = jax.vjp(norm_rows, states_f, gain_first)
    grad_state_norm, grad_gain_first = pull_first(grad_normed)
    grad_states = grad_middle + grad_state_norm
    kv_cols = key_full.shape[1]
    key_grad_full = lax.dynamic_update_slice_in_dim(
        jnp.zeros((feature_count, kv_cols), jnp.float32), grad_key, key_value_head * HEAD_SIZE, 1
    )
    value_grad_full = lax.dynamic_update_slice_in_dim(
        jnp.zeros((feature_count, kv_cols), jnp.float32), grad_value, key_value_head * HEAD_SIZE, 1
    )
    query_bias_full = lax.dynamic_update_slice_in_dim(
        jnp.zeros((bias_query.shape[0],), jnp.float32),
        grad_query_bias,
        tensor_split_index * head_cols,
        0,
    )
    key_bias_full = lax.dynamic_update_slice_in_dim(
        jnp.zeros((kv_cols,), jnp.float32), grad_key_bias, key_value_head * HEAD_SIZE, 0
    )
    value_bias_full = lax.dynamic_update_slice_in_dim(
        jnp.zeros((kv_cols,), jnp.float32), grad_value_bias, key_value_head * HEAD_SIZE, 0
    )
    big_sums = (
        lax.psum_scatter(
            grad_query.astype(jnp.bfloat16), "dp", scatter_dimension=0, tiled=True
        ).astype(jnp.float32),
        lax.psum_scatter(
            grad_output.astype(jnp.bfloat16), "dp", scatter_dimension=1, tiled=True
        ).astype(jnp.float32),
        lax.psum_scatter(
            grad_gate.astype(jnp.bfloat16), "dp", scatter_dimension=0, tiled=True
        ).astype(jnp.float32),
        lax.psum_scatter(
            grad_up.astype(jnp.bfloat16), "dp", scatter_dimension=0, tiled=True
        ).astype(jnp.float32),
        lax.psum_scatter(
            grad_down.astype(jnp.bfloat16), "dp", scatter_dimension=1, tiled=True
        ).astype(jnp.float32),
    )
    small_sums = (
        lax.psum_scatter(key_grad_full, ("dp", "tensor"), scatter_dimension=0, tiled=True),
        lax.psum_scatter(value_grad_full, ("dp", "tensor"), scatter_dimension=0, tiled=True),
        lax.psum_scatter(query_bias_full, ("dp", "tensor"), scatter_dimension=0, tiled=True),
        lax.psum_scatter(key_bias_full, ("dp", "tensor"), scatter_dimension=0, tiled=True),
        lax.psum_scatter(value_bias_full, ("dp", "tensor"), scatter_dimension=0, tiled=True),
        lax.psum_scatter(grad_gain_first, ("dp", "tensor"), scatter_dimension=0, tiled=True),
        lax.psum_scatter(grad_gain_second, ("dp", "tensor"), scatter_dimension=0, tiled=True),
    )
    return (
        result.astype(jnp.bfloat16),
        distill_loss,
        grad_states,
        big_sums[0],
        small_sums[0],
        small_sums[1],
        big_sums[1],
        big_sums[2],
        big_sums[3],
        big_sums[4],
        small_sums[2],
        small_sums[3],
        small_sums[4],
        small_sums[5],
        small_sums[6],
    )


def solution(mesh):
    placed = (
        P(("dp", "tensor"), None),
        P(("dp", "tensor"), None),
        P(("dp", "tensor"), None),
        P("dp"),
        P("dp", None),
        P("dp", "tensor"),
        P(("dp", "tensor"), None),
        P(("dp", "tensor"), None),
        P("tensor", "dp"),
        P("dp", "tensor"),
        P("dp", "tensor"),
        P("tensor", "dp"),
        P(("dp", "tensor")),
        P(("dp", "tensor")),
        P(("dp", "tensor")),
        P(("dp", "tensor")),
        P(("dp", "tensor")),
    )
    return jax.shard_map(
        body,
        mesh=mesh,
        in_specs=placed,
        out_specs=(
            P(("dp", "tensor"), None),
            P(),
            P(("dp", "tensor"), None),
            P("dp", "tensor"),
            P(("dp", "tensor"), None),
            P(("dp", "tensor"), None),
            P("tensor", "dp"),
            P("dp", "tensor"),
            P("dp", "tensor"),
            P("tensor", "dp"),
            P(("dp", "tensor")),
            P(("dp", "tensor")),
            P(("dp", "tensor")),
            P(("dp", "tensor")),
            P(("dp", "tensor")),
        ),
        check_vma=False,
    )
```

profile of v0, /device:TPU:0, one launch (start us, length us, event | category | flops | bytes accessed | tf_op | source)
XLA Modules:
  0.0 1583.3 jit_solution(15187255750521402281)
XLA Ops:
  12.2 42.7 %all-reduce.11 = (bf16[1536]{0:T(1024)(128)(2,1)S(1)}, bf16[1536]{0:T(1024)(128)(2,1)S(1)}, bf16[256]{0:T(256)(128)(2,1)S(1)}, bf16[256]{0:T(256)(128)(2,1)S(1)}, bf16[1536]{0:T(1024)(128)(2,1)S(1)}) all-reduce(bf16[1536]{0:T(1024)(128)(2,1)S(1)} %dynamic-update-slice, ...), channel_id=1, replica_groups=mesh['dp'=8,'tensor'=4] {'dp','tensor'}, use_global_device_ids=true, to_apply=%add | all-reduce | flops 5120 | bytes 20480
  60.6 3.0 fusion.75
  63.6 45.4 %all_gather.57 = bf16[1536,256]{1,0:T(8,128)(2,1)} all-gather(bf16[48,256]{1,0:T(8,128)(2,1)S(1)} %copy-done.28), channel_id=1, replica_groups=mesh['dp'=8,'tensor'=4] {'dp','tensor'}, dimensions={0}, use_global_device_ids=true | all-gather | bytes 811008 | tf_op jit(solution)/shard_map/all_gather | solution.py:75
  109.2 43.5 %all_gather.59 = bf16[1536,256]{1,0:T(8,128)(2,1)} all-gather(bf16[48,256]{1,0:T(8,128)(2,1)S(1)} %copy-done.29), channel_id=1, replica_groups=mesh['dp'=8,'tensor'=4] {'dp','tensor'}, dimensions={0}, use_global_device_ids=true | all-gather | bytes 811008 | tf_op jit(solution)/shard_map/all_gather | solution.py:76
  152.8 3.6 convolution_add_fusion
  174.3 20.0 %while.51 = (s32[]{:T(128)}, bf16[2,512,3,128]{3,1,2,0:T(8,128)(2,1)}, f32[2,3,512,1]{2,1,3,0:T(4,128)S(1)}, f32[2,3,512,1]{2,1,3,0:T(4,128)S(1)}, s32[2]{0:T(12...) while((s32[]{:T(128)}, ...), condition=%wide.region_4.5_spmd, body=%wide.region_1.4_spmd.sunk | while | flops 825949696 | bytes 29702440 | solution.py:148
  196.8 5.0 convolution_convert_fusion.4
  202.4 10.5 all-gather.16.cloned.1.call-start
  213.0 23.5 %reduce-scatter.12.cloned.1.call-done = bf16[256,1536]{1,0:T(8,128)(2,1)} async-done(((bf16[1024,1536]{1,0:T(8,128)(2,1)}), bf16[256,1536]{1,0:T(8,128)(2,1)}) %reduce-scatter.12.cloned.1.call-update) | async-done | bytes 786448 | tf_op jit(solution)/shard_map/reduce_scatter | solution.py:157
  241.8 105.0 %all-gather.18.cloned.1.call-done = bf16[1536,2240]{1,0:T(8,128)(2,1)} async-done(((bf16[192,2240]{1,0:T(8,128)(2,1)}), bf16[1536,2240]{1,0:T(8,128)(2,1)}) %all-gather.18.cloned.1.call-update) | async-done | bytes 6881296 | tf_op jit(solution)/shard_map/all_gather | solution.py:86
  346.8 28.7 %all-gather.16.cloned.1.call-done = bf16[1024,1536]{1,0:T(8,128)(2,1)} async-done(((bf16[256,1536]{1,0:T(8,128)(2,1)}), bf16[1024,1536]{1,0:T(8,128)(2,1)}) %all-gather.16.cloned.1.call-update) | async-done | bytes 3145744 | tf_op jit(solution)/shard_map/all_gather | solution.py:165
  375.6 13.2 fusion.96
  388.8 97.3 %all-gather.20.cloned.1.call-done = bf16[1536,2240]{1,0:T(8,128)(2,1)} async-done(((bf16[192,2240]{1,0:T(8,128)(2,1)}), bf16[1536,2240]{1,0:T(8,128)(2,1)}) %all-gather.20.cloned.1.call-update) | async-done | bytes 6881296 | tf_op jit(solution)/shard_map/all_gather | solution.py:87
  486.1 16.6 %multiply_convert_fusion.2 = (bf16[1024,2240]{0,1:T(8,128)(2,1)}, f32[1024,2240]{0,1:T(8,128)}) fusion(f32[1024,2240]{0,1:T(8,128)} %fusion.96, bf16[1024,1536]{1,0:T(8,128)(2,1)} %all-gather.16.cloned.1.call-done, bf16[1536,2240]{1,0:T(8,128)(2,1)} %all-gather.20.cloned.1.call-done), kind=kOutput, calls=%fused_computation.68 | convolution fusion | flops 7060193280 | bytes 32964608 | tf_op jit(solution)/shard_map/dot_general | solution.py:167
  502.7 92.1 %all-gather.22.cloned.1.call-done = bf16[2240,1536]{0,1:T(8,128)(2,1)} async-done(((bf16[2240,192]{0,1:T(8,128)(2,1)}), bf16[2240,1536]{0,1:T(8,128)(2,1)}) %all-gather.22.cloned.1.call-update) | async-done | bytes 6881296 | tf_op jit(solution)/shard_map/all_gather | solution.py:88
  594.8 12.4 convolution_convert_fusion.3
  607.9 38.8 %psum.15 = f32[]{:T(128)} all-reduce(f32[]{:T(128)} %get-tuple-element.384), channel_id=1, replica_groups=mesh['dp'=8,'tensor'=4] {'dp','tensor'}, use_global_device_ids=true, to_apply=%region_11.12 | all-reduce | flops 1 | bytes 8 | tf_op jit(solution)/shard_map/psum | solution.py:181
  650.1 29.5 %all-gather.24.cloned.1.call-done = bf16[1024,1536]{1,0:T(8,128)(2,1)} async-done(((bf16[256,1536]{1,0:T(8,128)(2,1)}), bf16[1024,1536]{1,0:T(8,128)(2,1)}) %all-gather.24.cloned.1.call-update) | async-done | bytes 3145744 | tf_op jit(solution)/shard_map/all_gather | solution.py:194
  679.6 20.9 %multiply_convert_fusion = (bf16[1024,2240]{0,1:T(8,128)(2,1)}, bf16[1024,2240]{0,1:T(8,128)(2,1)}) fusion(f32[1024,2240]{0,1:T(8,128)} %fusion.96, f32[1024,2240]{0,1:T(8,128)} %get-tuple-element.413, bf16[1024,1536]{1,0:T(8,128)(2,1)} %all-gather.24.cloned.1.call-done, bf16[2240,1536]{0,1:T(8,128)(2,1)} %all-gather.22.cloned.1.call-done), kind=kOutput, calls=%fused_computation.66 | convolution fusion | flops 7076249600 | bytes 37552128 | tf_op jit(solution)/shard_map/rd,fd->rf/dot_general | solution.py:195
  700.5 11.4 fusion.97
  711.9 11.6 add_convert_fusion.1
  723.5 38.0 %reduce-scatter.16.cloned.1.call-done = bf16[256,1536]{1,0:T(8,128)(2,1)} async-done(((bf16[1024,1536]{1,0:T(8,128)(2,1)}), bf16[256,1536]{1,0:T(8,128)(2,1)}) %reduce-scatter.16.cloned.1.call-update) | async-done | bytes 786448 | tf_op jit(solution)/shard_map/reduce_scatter | solution.py:210
  761.5 3.0 fusion.52
  767.3 28.6 %all-gather.26.cloned.1.call-done = bf16[1024,1536]{1,0:T(8,128)(2,1)} async-done(((bf16[256,1536]{1,0:T(8,128)(2,1)}), bf16[1024,1536]{1,0:T(8,128)(2,1)}) %all-gather.26.cloned.1.call-update) | async-done | bytes 3145744 | tf_op jit(solution)/shard_map/all_gather | solution.py:216
  795.8 5.0 convolution_convert_fusion.5
  800.9 3.3 convolution_convert_fusion.7
  804.3 52.2 %while.52 = (s32[]{:T(128)}, f32[1024,128]{1,0:T(8,128)}, f32[1024,128]{1,0:T(8,128)}, f32[2,512,3,128]{3,1,0,2:T(8,128)}, s32[2]{0:T(128)S(1)}, /*index=5*/s32[...) while((s32[]{:T(128)}, f32[1024,128]{1,0:T(8,128)}, ...), condition=%wide.region_16.17_spmd.clone, body=%wide.region_14.16_spmd.clone.sunk | while | flops 2031420416 | bytes 104920024 | solution.py:260
  805.8 3.7 fusion.166
  812.6 5.6 fusion.168
  825.5 4.7 fusion.171
  831.6 3.7 fusion.166
  838.4 5.6 fusion.168
  848.5 3.0 fusion.170
  851.5 5.0 fusion.171
  863.0 4.0 convolution_convert_fusion.6
  867.1 12.6 convolution_convert_fusion
  879.8 12.4 convolution_convert_fusion.2
  892.3 12.4 convolution_convert_fusion.1
  913.2 3.7 add_convert_fusion
  921.6 3.0 convolution_dynamic-update-slice_fusion
  928.8 5.0 reduce-scatter.20.cloned.1.call-done
  935.4 129.9 %reduce-scatter.32.cloned.1.call-done = bf16[2240,192]{0,1:T(8,128)(2,1)} async-done(((bf16[2240,1536]{0,1:T(8,128)(2,1)}), bf16[2240,192]{0,1:T(8,128)(2,1)}) %reduce-scatter.32.cloned.1.call-update) | async-done | bytes 860176 | tf_op jit(solution)/shard_map/reduce_scatter | solution.py:335
  1067.8 129.3 %reduce-scatter.28.cloned.1.call-done = bf16[192,2240]{1,0:T(8,128)(2,1)} async-done(((bf16[1536,2240]{1,0:T(8,128)(2,1)}), bf16[192,2240]{1,0:T(8,128)(2,1)}) %reduce-scatter.28.cloned.1.call-update) | async-done | bytes 860176 | tf_op jit(solution)/shard_map/reduce_scatter | solution.py:329
  1199.6 129.4 %reduce-scatter.30.cloned.1.call-done = bf16[192,2240]{1,0:T(8,128)(2,1)} async-done(((bf16[1536,2240]{1,0:T(8,128)(2,1)}), bf16[192,2240]{1,0:T(8,128)(2,1)}) %reduce-scatter.30.cloned.1.call-update) | async-done | bytes 860176 | tf_op jit(solution)/shard_map/reduce_scatter | solution.py:332
  1331.5 37.0 %reduce-scatter.18.cloned.1.call-done = bf16[256,1536]{1,0:T(8,128)(2,1)} async-done(((bf16[1024,1536]{1,0:T(8,128)(2,1)}), bf16[256,1536]{1,0:T(8,128)(2,1)}) %reduce-scatter.18.cloned.1.call-update) | async-done | bytes 786448 | tf_op jit(solution)/shard_map/reduce_scatter | solution.py:297
  1370.3 40.1 %all-reduce.10 = (f32[]{:T(128)}, f32[1536]{0:T(1024)S(1)}, f32[256]{0:T(256)S(1)}, f32[256]{0:T(256)S(1)}, f32[1536]{0:T(1024)S(1)}, /*index=5*/f32[1536]{0:T(1024)S(1)}) all-reduce(f32[]{:T(128)} %get-tuple-element.320, f32[1536]{0:T(1024)S(1)} %bitcast_dynamic-update-slice_fusion.2, ...), channel_id=1, replica_groups=mesh['dp'=8,'tensor'=4] {'dp','tensor'}, use_global_device_ids=true, to_apply=%region_9.10 | all-reduce | flops 5121 | bytes 40968 | tf_op jit(solution)/shard_map/psum | solution.py:181
  1416.7 55.5 %reduce-scatter.22.cloned.1.call-done = f32[48,256]{1,0:T(8,128)} async-done(((f32[1536,256]{1,0:T(8,128)}), f32[48,256]{1,0:T(8,128)}) %reduce-scatter.22.cloned.1.call-update) | async-done | bytes 49168 | tf_op jit(solution)/shard_map/reduce_scatter | solution.py:340
  1472.2 102.7 %reduce-scatter.24.cloned.1.call-done = f32[48,256]{1,0:T(8,128)} async-done(((f32[1536,256]{1,0:T(8,128)}), f32[48,256]{1,0:T(8,128)}) %reduce-scatter.24.cloned.1.call-update) | async-done | bytes 49168 | tf_op jit(solution)/shard_map/reduce_scatter | solution.py:341
  (255 shorter events, 117.1 us)
Async XLA Ops:
  7.2 56.4 %copy-start.28 = (bf16[48,256]{1,0:T(8,128)(2,1)S(1)}, bf16[48,256]{1,0:T(8,128)(2,1)}, u32[]{:S(2)}) copy-start(bf16[48,256]{1,0:T(8,128)(2,1)} %param.27) | copy-start | bytes 73732
  7.2 102.0 %copy-start.29 = (bf16[48,256]{1,0:T(8,128)(2,1)S(1)}, bf16[48,256]{1,0:T(8,128)(2,1)}, u32[]{:S(2)}) copy-start(bf16[48,256]{1,0:T(8,128)(2,1)} %param.28) | copy-start | bytes 73732
  7.2 145.6 %all-gather.12.cloned.1.call-start = ((), (), s32[]{:S(2)}) async-start(), calls=%async_computation.12 | async-start | bytes 1327104 | tf_op jit(solution)/shard_map/all_gather | solution.py:84
  7.9 144.9 %all-gather.10.cloned.1.call-start = ((), (), s32[]{:S(2)}) async-start(), calls=%async_computation.11 | async-start | bytes 3932160 | tf_op jit(solution)/shard_map/all_gather | solution.py:106
  59.8 137.0 %all-gather.14.cloned.1.call-start = ((), (), s32[]{:S(2)}) async-start(), calls=%async_computation.13 | async-start | bytes 1327104 | tf_op jit(solution)/shard_map/all_gather | solution.py:85
  60.5 176.0 %reduce-scatter.12.cloned.1.call-start = ((), (), s32[]{:S(2)}) async-start(), calls=%async_computation.14 | async-start | bytes 3932160 | tf_op jit(solution)/shard_map/reduce_scatter | solution.py:157
  60.6 105.0 %copy-start.34 = (f32[64]{0:T(128)}, f32[64]{0:T(128)S(1)}, u32[]{:S(2)}) copy-start(f32[64]{0:T(128)S(1)} %negate_power_fusion) | copy-start | bytes 772
  157.8 5.7 copy-start.3
  196.8 5.1 copy-start.21
  201.8 34.7 %copy-start.1 = (bf16[256,1536]{1,0:T(8,128)(2,1)S(1)}, bf16[256,1536]{1,0:T(8,128)(2,1)}, u32[]{:S(2)}) copy-start(bf16[256,1536]{1,0:T(8,128)(2,1)} %param.21) | copy-start | bytes 2359300
  201.8 145.0 %all-gather.18.cloned.1.call-start = ((), (), s32[]{:S(2)}) async-start(), calls=%async_computation.16 | async-start | bytes 7962624 | tf_op jit(solution)/shard_map/all_gather | solution.py:86
  202.4 173.1 %all-gather.16.cloned.1.call-start = ((), (), s32[]{:S(2)}) async-start(), calls=%async_computation.15 | async-start | bytes 3932160 | tf_op jit(solution)/shard_map/all_gather | solution.py:165
  240.3 245.8 %all-gather.20.cloned.1.call-start = ((), (), s32[]{:S(2)}) async-start(), calls=%async_computation.17 | async-start | bytes 7962624 | tf_op jit(solution)/shard_map/all_gather | solution.py:87
  241.0 353.7 %all-gather.22.cloned.1.call-start = ((), (), s32[]{:S(2)}) async-start(), calls=%async_computation.18 | async-start | bytes 7962624 | tf_op jit(solution)/shard_map/all_gather | solution.py:88
  241.8 405.7 %reduce-scatter.14.cloned.1.call-start = ((), (), s32[]{:S(2)}) async-start(), calls=%async_computation.19 | async-start | bytes 3932160 | tf_op jit(solution)/shard_map/reduce_scatter | solution.py:170
  607.2 40.3 %copy-start.5 = (bf16[256,1536]{1,0:T(8,128)(2,1)S(1)}, bf16[256,1536]{1,0:T(8,128)(2,1)}, u32[]{:S(2)}) copy-start(bf16[256,1536]{1,0:T(8,128)(2,1)} %reduce-scatter.12.cloned.1.call-done) | copy-start | bytes 2359300
  607.2 40.3 %copy-start.8 = (bf16[256,1536]{1,0:T(8,128)(2,1)S(1)}, bf16[256,1536]{1,0:T(8,128)(2,1)}, u32[]{:S(2)}) copy-start(bf16[256,1536]{1,0:T(8,128)(2,1)} %param.23) | copy-start | bytes 2359300
  607.2 40.3 %copy-start.15 = (bf16[256,1536]{1,0:T(8,128)(2,1)S(1)}, bf16[256,1536]{1,0:T(8,128)(2,1)}, u32[]{:S(2)}) copy-start(bf16[256,1536]{1,0:T(8,128)(2,1)} %param.22) | copy-start | bytes 2359300
  607.2 72.4 %all-gather.24.cloned.1.call-start = ((), (), s32[]{:S(2)}) async-start(), calls=%async_computation.20 | async-start | bytes 3932160 | tf_op jit(solution)/shard_map/all_gather | solution.py:194
  650.1 111.4 %reduce-scatter.16.cloned.1.call-start = ((), (), s32[]{:S(2)}) async-start(), calls=%async_computation.21 | async-start | bytes 3932160 | tf_op jit(solution)/shard_map/reduce_scatter | solution.py:210
  700.5 11.4 copy-start.37
  723.5 38.1 %copy-start.9 = (bf16[256,1536]{1,0:T(8,128)(2,1)S(1)}, bf16[256,1536]{1,0:T(8,128)(2,1)}, u32[]{:S(2)}) copy-start(bf16[256,1536]{1,0:T(8,128)(2,1)} %reduce-scatter.14.cloned.1.call-done) | copy-start | bytes 2359300
  723.5 72.4 %all-gather.26.cloned.1.call-start = ((), (), s32[]{:S(2)}) async-start(), calls=%async_computation.22 | async-start | bytes 3932160 | tf_op jit(solution)/shard_map/all_gather | solution.py:216
  767.2 160.0 %reduce-scatter.26.cloned.1.call-start = ((), (), s32[]{:S(2)}) async-start(), calls=%async_computation.27 | async-start | bytes 1327104 | tf_op jit(solution)/shard_map/reduce_scatter | solution.py:326
  767.3 33.7 %copy-start.36 = (bf16[384,1536]{0,1:T(8,128)(2,1)S(1)}, bf16[384,1536]{0,1:T(8,128)(2,1)}, u32[]{:S(2)}) copy-start(bf16[384,1536]{0,1:T(8,128)(2,1)} %all-gather.14.cloned.1.call-done) | copy-start | bytes 3538948
  800.9 132.9 %reduce-scatter.20.cloned.1.call-start = ((), (), s32[]{:S(2)}) async-start(), calls=%async_computation.24 | async-start | bytes 1327104 | tf_op jit(solution)/shard_map/reduce_scatter | solution.py:323
  804.5 5.0 copy-start.6
  812.6 5.6 slice-start
  812.6 5.6 slice-start.1
  825.5 4.8 copy-start.7
  825.5 4.8 copy-start.12
  830.3 5.0 copy-start.6
  838.4 5.6 slice-start
  838.4 5.6 slice-start.1
  851.5 5.0 copy-start.7
  851.5 5.0 copy-start.12
  867.1 198.2 %reduce-scatter.32.cloned.1.call-start = ((), (), s32[]{:S(2)}) async-start(), calls=%async_computation.30 | async-start | bytes 7962624 | tf_op jit(solution)/shard_map/reduce_scatter | solution.py:335
  879.7 317.4 %reduce-scatter.28.cloned.1.call-start = ((), (), s32[]{:S(2)}) async-start(), calls=%async_computation.28 | async-start | bytes 7962624 | tf_op jit(solution)/shard_map/reduce_scatter | solution.py:329
  892.2 436.7 %reduce-scatter.30.cloned.1.call-start = ((), (), s32[]{:S(2)}) async-start(), calls=%async_computation.29 | async-start | bytes 7962624 | tf_op jit(solution)/shard_map/reduce_scatter | solution.py:332
  904.7 463.7 %reduce-scatter.18.cloned.1.call-start = ((), (), s32[]{:S(2)}) async-start(), calls=%async_computation.23 | async-start | bytes 3932160 | tf_op jit(solution)/shard_map/reduce_scatter | solution.py:297
  917.0 555.2 %reduce-scatter.22.cloned.1.call-start = ((), (), s32[]{:S(2)}) async-start(), calls=%async_computation.25 | async-start | bytes 1622016 | tf_op jit(solution)/shard_map/reduce_scatter | solution.py:340
  920.3 654.5 %reduce-scatter.24.cloned.1.call-start = ((), (), s32[]{:S(2)}) async-start(), calls=%async_computation.26 | async-start | bytes 1622016 | tf_op jit(solution)/shard_map/reduce_scatter | solution.py:341
  1067.8 300.6 %copy-start.2 = (bf16[256,1536]{1,0:T(8,128)(2,1)S(1)}, bf16[256,1536]{1,0:T(8,128)(2,1)}, u32[]{:S(2)}) copy-start(bf16[256,1536]{1,0:T(8,128)(2,1)} %param.21) | copy-start | bytes 2359300
  1067.8 300.6 %copy-start.26 = (f32[1536]{0:T(1024)S(1)}, f32[1536]{0:T(1024)}, u32[]{:S(2)}) copy-start(f32[1536]{0:T(1024)} %copy-done.25) | copy-start | bytes 18436
  1067.8 300.6 %copy-start.31 = (f32[256]{0:T(256)S(1)}, f32[256]{0:T(256)}, u32[]{:S(2)}) copy-start(f32[256]{0:T(256)} %copy-done.30) | copy-start | bytes 3076
  1067.8 302.4 %copy-start.27 = (f32[1536]{0:T(1024)S(1)}, f32[1536]{0:T(1024)}, u32[]{:S(2)}) copy-start(f32[1536]{0:T(1024)} %get-tuple-element.318) | copy-start | bytes 18436
  1067.8 346.1 %copy-start.33 = (f32[256]{0:T(256)S(1)}, f32[256]{0:T(256)}, u32[]{:S(2)}) copy-start(f32[256]{0:T(256)} %copy-done.32) | copy-start | bytes 3076
  1067.8 346.1 %copy-start.13 = (f32[256,1536]{1,0:T(8,128)S(1)}, f32[256,1536]{1,0:T(8,128)}, u32[]{:S(2)}) copy-start(f32[256,1536]{1,0:T(8,128)} %get-tuple-element.383) | copy-start | bytes 4718596
  (21 other events, 46.3 us)
Sparse Core Ops, SparseCore 0:
  10.2 43.9 all-gather.11
  59.9 33.2 all-gather.9
  95.4 41.3 all-gather.13
  202.0 34.4 reduce-scatter.11
  238.5 108.2 all-gather.17
  348.8 26.6 all-gather.15
  377.7 108.2 all-gather.19
  488.2 106.4 all-gather.21
  607.3 36.1 reduce-scatter.13
  650.2 29.3 all-gather.23
  723.6 37.8 reduce-scatter.15
  767.3 28.4 all-gather.25
  801.0 64.8 reduce-scatter.25
  869.7 64.0 reduce-scatter.19
  937.3 127.9 reduce-scatter.31
  1068.8 128.2 reduce-scatter.27
  1200.7 128.2 reduce-scatter.29
  1331.4 37.0 reduce-scatter.17
  1374.2 97.8 reduce-scatter.21
  1477.8 97.0 reduce-scatter.23
where the time goes:
time: 1590 us; the launch traced here: 1580 us
  waiting for transfers between devices  1030 us (65%)
  blocking collectives  211 us (13%)
  matrix products  208 us (13%)
  other arithmetic  58 us (4%)
  local copies, waits for them, and re-layouts  34.8 us (2%)
  between operations  18.4 us (1%)
    reduce_scatter x1, waiting for transfers between devices, body(): lax.psum_scatter(grad_down.astype(jnp.bfloat16), 'dp', scatter_dimension=...  130 us
    reduce_scatter x1, waiting for transfers between devices, body(): lax.psum_scatter(grad_up.astype(jnp.bfloat16), 'dp', scatter_dimension=0,...  129 us
    reduce_scatter x1, waiting for transfers between devices, body(): lax.psum_scatter(grad_gate.astype(jnp.bfloat16), 'dp', scatter_dimension=...  129 us
    all_gather x1, waiting for transfers between devices, body(): lax.all_gather(w_gate, 'dp', axis=0, tiled=True)  105 us
    reduce_scatter x1, waiting for transfers between devices, body(): lax.psum_scatter(value_grad_full, ('dp', 'tensor'), scatter_dimension=0,...  103 us
    all_gather x1, waiting for transfers between devices, body(): lax.all_gather(w_up, 'dp', axis=0, tiled=True)  97.3 us
    all_gather x1, waiting for transfers between devices, body(): lax.all_gather(w_down, 'dp', axis=1, tiled=True)  92.1 us
    psum x2, blocking collectives, body(): lax.psum((jnp.sum(valid_rows * deviation * deviation), jnp.sum(valid_rows...  78.9 us
  transfers between devices with their start and end apart: 20, of which 15 were waited for; matrix products, arithmetic and copies ran while one was open for 14% of the time, Pallas kernels for 0%

commit v1 on v0

v1 whole, which is shorter than its diff:
```python
import functools

import jax
import jax.numpy as jnp
from jax import lax
from jax.experimental import pallas as pl
from jax.experimental.pallas import tpu as pltpu
from jax.sharding import PartitionSpec as P

QUERY_HEADS = 12
KEY_VALUE_HEADS = 2
HEAD_SIZE = 128

NORM_EPS = 1e-06
ROPE_BASE = 10000.0
NEG_FILL = -1e30

F32 = jnp.float32
BF16 = jnp.bfloat16


def mm(spec, left, right):
    return jnp.einsum(spec, left, right, preferred_element_type=F32)


def tables(positions):
    half_width = HEAD_SIZE // 2
    inverse = ROPE_BASE ** (-(jnp.arange(half_width, dtype=F32) * 2.0 / HEAD_SIZE))
    angles = positions.astype(F32)[:, None] * inverse[None, :]
    return jnp.cos(angles), jnp.sin(angles)


def rotate(values, cosine, sine):
    half_width = values.shape[-1] // 2
    first = values[..., :half_width]
    second = values[..., half_width:]
    return jnp.concatenate(
        [first * cosine - second * sine, second * cosine + first * sine], axis=-1
    )


def after(value, *tokens):
    return lax.optimization_barrier((value,) + tokens)[0]


def swap(value, axis, size, bits):
    return lax.ppermute(value, axis, [(i, i ^ bits) for i in range(size)])


def ring_position(index, size):
    return jnp.where(index % 2 == 0, index // 2, size - (index + 1) // 2)


def ring_member(position, size):
    position = position % size
    return jnp.where(position < size // 2, 2 * position, 2 * (size - position) - 1)


def ring_pairs(size, step):
    ring = list(range(0, size, 2)) + list(range(size - 1, 0, -2))
    return [(ring[i], ring[(i + step) % size]) for i in range(size)]


class Gather:
    def __init__(self, shard, size):
        self.size = size
        self.shard = shard
        self.up = self.down = shard
        self.ups, self.downs = [], []
        self.steps = size // 2
        self.done = 0

    def step(self, *tokens):
        size, rows = self.size, self.shard.shape[0]
        up, down = self.up, self.down
        if self.done == self.steps - 1:
            up, down = up[: rows // 2], down[rows // 2 :]
        if tokens:
            up, down = lax.optimization_barrier((up, down) + tokens)[:2]
        self.up = lax.ppermute(up, "dp", ring_pairs(size, 1))
        self.down = lax.ppermute(down, "dp", ring_pairs(size, -1))
        self.ups.append(self.up)
        self.downs.append(self.down)
        self.done += 1
        return self.up, self.down

    def whole(self):
        size = self.size
        rows, cols = self.shard.shape
        mine = ring_position(lax.axis_index("dp"), size)
        count = self.steps
        from_up = [ring_member(mine - k, size) for k in range(1, count + 1)]
        from_down = [ring_member(mine + k, size) for k in range(1, count + 1)]
        where = jnp.stack([lax.axis_index("dp")] + from_up + from_down).astype(jnp.int32)
        blocks = [self.shard] + self.ups + self.downs
        spans = [(0, rows)] + ([(0, rows)] * (count - 1) + [(0, rows // 2)])
        spans += [(0, rows)] * (count - 1) + [(rows // 2, rows - rows // 2)]
        return place(blocks, spans, where, size).reshape(size * rows, cols)


def place_kernel(spans, where, *refs):
    blocks, (out, sem) = refs[: len(spans)], refs[len(spans) :]
    copies = []
    for k, (start, length) in enumerate(spans):
        copies.append(
            pltpu.make_async_copy(
                blocks[k], out.at[where[k], pl.ds(start, length)], sem.at[k]
            )
        )
    for copy in copies:
        copy.start()
    for copy in copies:
        copy.wait()


def place(blocks, spans, where, size):
    rows, cols = blocks[0].shape
    anywhere = pl.BlockSpec(memory_space=pl.ANY)
    return pl.pallas_call(
        functools.partial(place_kernel, spans),
        out_shape=jax.ShapeDtypeStruct((size, rows, cols), blocks[0].dtype),
        in_specs=[pl.BlockSpec(memory_space=pltpu.SMEM)] + [anywhere] * len(blocks),
        out_specs=anywhere,
        scratch_shapes=[pltpu.SemaphoreType.DMA((len(blocks),))],
    )(where, *blocks)


class Scatter:
    def __init__(self, blocks, size):
        self.blocks, self.size = blocks, size
        self.mine = ring_position(lax.axis_index("dp"), size)
        self.rows = blocks.shape[1]
        self.left = size // 2
        self.up = self.down = None

    def block(self, offset):
        return lax.dynamic_index_in_dim(
            self.blocks, ring_member(self.mine + offset, self.size), 0, keepdims=False
        )

    def step(self, *tokens):
        half = self.rows // 2
        if self.up is None:
            up = self.block(self.left)
            up, down = up[:half], up[half:]
        else:
            up, down = self.block(self.left), self.block(-self.left)
            if self.left == self.size // 2 - 1:
                up = jnp.concatenate([add16(up[:half], self.up), up[half:]])
                down = jnp.concatenate([down[:half], add16(down[half:], self.down)])
            else:
                up, down = add16(up, self.up), add16(down, self.down)
        if tokens:
            up, down = lax.optimization_barrier((up, down) + tokens)[:2]
        self.up = lax.ppermute(up, "dp", ring_pairs(self.size, 1))
        self.down = lax.ppermute(down, "dp", ring_pairs(self.size, -1))
        self.left -= 1
        return self.up, self.down

    def result(self):
        own = lax.dynamic_index_in_dim(self.blocks, lax.axis_index("dp"), 0, keepdims=False)
        return own.astype(F32) + self.up.astype(F32) + self.down.astype(F32)


def add16(left, right):
    return (left.astype(F32) + right.astype(F32)).astype(BF16)


def gather_rows(rows):
    across = swap(rows, "tensor", 4, 2)
    beside = swap(rows, "tensor", 4, 1)
    corner = swap(across, "tensor", 4, 1)
    return jnp.concatenate([rows, beside, across, corner], 0)


def scatter_rows(far, near):
    rows = far.shape[0] // 2
    far_in = swap(far[rows:], "tensor", 4, 1)
    far_sum = add16(far[:rows], far_in)
    across = swap(far_sum, "tensor", 4, 2)
    near_in = swap(near[rows:], "tensor", 4, 1)
    return near[:rows].astype(F32) + near_in.astype(F32) + across.astype(F32)


def gather_small(vector, size):
    block = vector[None]
    for bit in (1, 2):
        block = jnp.concatenate([block, swap(block, "tensor", 4, bit)], 0)
    bit = 1
    while bit < size:
        block = jnp.concatenate([block, swap(block, "dp", size, bit)], 0)
        bit *= 2
    me = lax.axis_index("dp") * 4 + lax.axis_index("tensor")
    order = jnp.arange(size * 4, dtype=jnp.int32) ^ me
    return jnp.take(block, order, axis=0)


def sum_small(block, size):
    for bit in (1, 2):
        block = block + swap(block, "tensor", 4, bit)
    bit = 1
    while bit < size:
        block = block + swap(block, "dp", size, bit)
        bit *= 2
    return block


def attend(queries, keys, values, allowed, scale):
    outs, saved = [], []
    for low, high in ((0, 512), (512, 1024)):
        scores = mm("qhd,kd->hqk", queries[low:high], keys) * scale
        scores = jnp.where(allowed[None, low:high], scores, NEG_FILL)
        row_max = jnp.max(scores, -1, keepdims=True)
        shifted = jnp.exp(scores - row_max)
        row_sum = jnp.sum(shifted, -1, keepdims=True)
        low_probs = (shifted / row_sum).astype(BF16)
        outs.append(mm("hqk,kd->qhd", low_probs, values).astype(BF16))
        saved.append((row_max, row_sum))
    return jnp.concatenate(outs, 0), saved


def attend_back(queries, keys, values, grads, allowed, scale, saved):
    grad_queries, grad_keys, grad_values = [], 0.0, 0.0
    for (low, high), (row_max, row_sum) in zip(((0, 512), (512, 1024)), saved):
        query, grad = queries[low:high], grads[low:high]
        scores = mm("qhd,kd->hqk", query, keys) * scale
        scores = jnp.where(allowed[None, low:high], scores, NEG_FILL)
        probs = jnp.exp(scores - row_max) / row_sum
        grad_probs = mm("qhd,kd->hqk", grad, values)
        spread = jnp.sum(probs * grad_probs, -1, keepdims=True)
        grad_scores = (probs * (grad_probs - spread)).astype(BF16)
        grad_queries.append(mm("hqk,kd->qhd", grad_scores, keys) * scale)
        grad_keys = grad_keys + mm("hqk,qhd->kd", grad_scores, query) * scale
        grad_values = grad_values + mm("hqk,qhd->kd", probs.astype(BF16), grad)
    return jnp.concatenate(grad_queries, 0), grad_keys, grad_values


def body(
    states,
    cotangent,
    teacher,
    prefix_len,
    validity,
    w_query,
    key_projection_weight,
    value_projection_weight,
    w_output,
    w_gate,
    w_up,
    w_down,
    b_query,
    key_offset_bias,
    value_offset_bias,
    gain_attn,
    gain_ffn,
):
    groups = lax.axis_size("tensor")
    dp_size = lax.axis_size("dp")
    tensor_index = lax.axis_index("tensor")
    dp_index = lax.axis_index("dp")
    row_count, feature_count = states.shape
    all_rows = row_count * groups
    local_heads = QUERY_HEADS // groups
    head_cols = local_heads * HEAD_SIZE
    kv_head = tensor_index * local_heads // (QUERY_HEADS // KEY_VALUE_HEADS)
    score_scale = HEAD_SIZE ** (-0.5)
    shard_rows = w_query.shape[0]

    blocks = [tensor_index ^ r for r in range(groups)]
    positions = jnp.concatenate(
        [b * row_count + jnp.arange(row_count, dtype=jnp.int32) for b in blocks]
    )
    valid_seq = validity.reshape(groups, row_count)
    valid_all = jnp.concatenate(
        [lax.dynamic_index_in_dim(valid_seq, b, 0, keepdims=False) for b in blocks]
    )
    valid_rows = valid_all[:row_count].astype(F32)[:, None]

    bias_part, kv_part = b_query.shape[0], key_offset_bias.shape[0]
    seq_count = jnp.sum(validity).astype(F32)[None]
    small = jnp.concatenate(
        [
            b_query.astype(F32),
            gain_attn.astype(F32),
            gain_ffn.astype(F32),
            key_offset_bias.astype(F32),
            value_offset_bias.astype(F32),
            seq_count,
        ]
    )
    small = gather_small(small, dp_size)
    at = 0
    pieces = []
    for width in (bias_part, bias_part, bias_part, kv_part, kv_part, 1):
        pieces.append(small[:, at : at + width].reshape(-1))
        at += width
    bias_query, gain_one, gain_two, bias_key, bias_value, counts = pieces
    count_all = jnp.sum(counts) / groups
    query_bias = lax.dynamic_slice_in_dim(bias_query, tensor_index * head_cols, head_cols, 0)
    key_bias = lax.dynamic_slice_in_dim(bias_key, kv_head * HEAD_SIZE, HEAD_SIZE, 0)
    value_bias = lax.dynamic_slice_in_dim(bias_value, kv_head * HEAD_SIZE, HEAD_SIZE, 0)
    qkv_bias = jnp.concatenate([query_bias, key_bias, value_bias])

    kv = jnp.concatenate(
        [
            key_projection_weight.reshape(-1, KEY_VALUE_HEADS, HEAD_SIZE),
            value_projection_weight.reshape(-1, KEY_VALUE_HEADS, HEAD_SIZE),
        ],
        -1,
    )
    kv_own = lax.dynamic_index_in_dim(kv, kv_head, 1, keepdims=False)
    kv_other = lax.dynamic_index_in_dim(kv, 1 - kv_head, 1, keepdims=False)
    kv_pair = jnp.stack([kv_own, swap(kv_other, "tensor", 4, 2)])
    kv_beside = swap(kv_pair, "tensor", 4, 1)
    kv_rel = jnp.stack([kv_pair[0], kv_beside[0], kv_pair[1], kv_beside[1]])
    kv_rows = jnp.take(kv_rel, jnp.arange(groups, dtype=jnp.int32) ^ tensor_index, axis=0)
    kv_rows = kv_rows.reshape(shard_rows, 2 * HEAD_SIZE)

    states_all = gather_rows(states)
    ring_q = Gather(w_query, dp_size)
    ring_kv = Gather(kv_rows, dp_size)
    ring_o = Gather(w_output.T, dp_size)
    ring_gate = Gather(w_gate, dp_size)
    ring_up = Gather(w_up, dp_size)
    ring_down = Gather(w_down.T, dp_size)
    window = []

    def go(ring, steps):
        for _ in range(steps):
            tokens = window[-2] if len(window) >= 2 else ()
            window.append(ring.step(*tokens))

    steps = dp_size // 2
    for _ in range(steps):
        ring_q.step()
        ring_kv.step()
        ring_o.step()
    window.append(ring_q.ups[-2:-1])
    for _ in range(steps):
        go(ring_gate, 1)
        go(ring_up, 1)
    go(ring_down, steps)

    states_f = states_all.astype(F32)
    rms_one = lax.rsqrt(jnp.mean(states_f * states_f, -1, keepdims=True) + NORM_EPS)
    normed_all = (states_f * rms_one * gain_one).astype(BF16)
    w_qkv = jnp.concatenate([ring_q.whole(), ring_kv.whole()], 1)
    qkv = jnp.dot(normed_all, w_qkv, preferred_element_type=F32) + qkv_bias
    cosine, sine = tables(positions)
    queries = rotate(
        qkv[:, :head_cols].reshape(all_rows, local_heads, HEAD_SIZE),
        cosine[:, None, :],
        sine[:, None, :],
    ).astype(BF16)
    keys = rotate(qkv[:, head_cols : head_cols + HEAD_SIZE], cosine, sine).astype(BF16)
    values = qkv[:, head_cols + HEAD_SIZE :].astype(BF16)
    allowed = (positions[None, :] <= positions[:, None]) | (positions[None, :] < prefix_len[0])
    allowed = allowed & (valid_all[None, :] > 0)
    attended, saved = attend(queries, keys, values, allowed, score_scale)
    attended = attended.reshape(all_rows, head_cols)
    output_t = ring_o.whole()
    half = all_rows // 2
    far = mm("rh,dh->rd", attended[half:], output_t).astype(BF16)
    near = mm("rh,dh->rd", attended[:half], output_t).astype(BF16)
    states_own = states_f[:row_count]
    middle = states_own + scatter_rows(far, near)

    rms_two = lax.rsqrt(jnp.mean(middle * middle, -1, keepdims=True) + NORM_EPS)
    normed_two = (middle * rms_two * gain_two).astype(BF16)
    normed_two_all = gather_rows(normed_two)
    gate_w, up_w = ring_gate.whole(), ring_up.whole()
    gate_act = jnp.dot(normed_two_all, gate_w, preferred_element_type=F32)
    up_act = jnp.dot(normed_two_all, up_w, preferred_element_type=F32)
    sigma = jax.nn.sigmoid(gate_act)
    hidden = (gate_act * sigma * up_act).astype(BF16)
    down_t = ring_down.whole()
    far = mm("rf,df->rd", hidden[half:], down_t).astype(BF16)
    near = mm("rf,df->rd", hidden[:half], down_t).astype(BF16)
    result = middle + scatter_rows(far, near)

    deviation = result - teacher.astype(F32)
    square_sum = jnp.sum(valid_rows * deviation * deviation)
    token_total = float(all_rows * dp_size)
    grad_result = cotangent.astype(F32) + token_total / count_all * valid_rows * deviation

    grad_two_all = gather_rows(grad_result.astype(BF16))

    def split(gradient):
        return gradient.astype(BF16).reshape(dp_size, shard_rows, -1)

    grad_down = mm("rd,rf->df", grad_two_all, hidden)
    sum_down = Scatter(split(grad_down), dp_size)
    grad_hidden = mm("rd,df->rf", grad_two_all, down_t)
    grad_gate_act = (grad_hidden * up_act * sigma * (1.0 + gate_act * (1.0 - sigma))).astype(BF16)
    grad_up_act = (grad_hidden * gate_act * sigma).astype(BF16)
    sum_gate = Scatter(split(mm("rd,rf->df", normed_two_all, grad_gate_act)), dp_size)
    sum_up = Scatter(split(mm("rd,rf->df", normed_two_all, grad_up_act)), dp_size)
    far = mm("rf,df->rd", grad_gate_act[half:], gate_w)
    far = (far + mm("rf,df->rd", grad_up_act[half:], up_w)).astype(BF16)
    near = mm("rf,df->rd", grad_gate_act[:half], gate_w)
    near = (near + mm("rf,df->rd", grad_up_act[:half], up_w)).astype(BF16)
    grad_normed_two = scatter_rows(far, near)
    scaled_two = middle * rms_two
    grad_gain_two = jnp.sum(grad_normed_two * scaled_two, 0)
    pulled = gain_two * grad_normed_two
    grad_middle = grad_result + rms_two * (
        pulled - scaled_two * jnp.mean(pulled * scaled_two, -1, keepdims=True)
    )
    grad_one_all = gather_rows(grad_middle.astype(BF16))
    sum_o = Scatter(split(mm("rd,rh->dh", grad_one_all, attended)), dp_size)
    grad_attended = mm("rd,dh->rh", grad_one_all, output_t).astype(BF16)
    grad_queries, grad_keys, grad_values = attend_back(
        queries,
        keys,
        values,
        grad_attended.reshape(all_rows, local_heads, HEAD_SIZE),
        allowed,
        score_scale,
        saved,
    )
    grad_query_raw = rotate(grad_queries, cosine[:, None, :], -sine[:, None, :]).astype(BF16)
    grad_key_raw = rotate(grad_keys, cosine, -sine).astype(BF16)
    grad_qkv = jnp.concatenate(
        [grad_query_raw.reshape(all_rows, head_cols), grad_key_raw, grad_values.astype(BF16)], 1
    )
    sum_qkv = Scatter(split(mm("rd,rf->df", normed_all, grad_qkv)), dp_size)
    grad_qkv_bias = jnp.sum(grad_qkv.astype(F32), 0)
    grad_normed_part = mm("rf,df->rd", grad_qkv, w_qkv)
    scaled_one = states_f * rms_one
    grad_gain_one = jnp.sum(grad_normed_part * scaled_one, 0)
    grad_normed_part = grad_normed_part.astype(BF16)
    grad_normed = scatter_rows(grad_normed_part[half:], grad_normed_part[:half])
    pulled = gain_one * grad_normed
    scaled_own = scaled_one[:row_count]
    grad_states = grad_middle + rms_one[:row_count] * (
        pulled - scaled_own * jnp.mean(pulled * scaled_own, -1, keepdims=True)
    )

    window.clear()

    def send(ring, steps):
        for _ in range(steps):
            tokens = window[-2] if len(window) >= 2 else ()
            window.append(ring.step(*tokens))

    send(sum_down, 1)
    send(sum_down, 1)
    for _ in range(steps - 2):
        send(sum_down, 1)
        send(sum_gate, 1)
    send(sum_gate, 1)
    send(sum_up, 1)
    send(sum_gate, 1)
    send(sum_up, 1)
    for _ in range(steps - 2):
        send(sum_up, 1)
        send(sum_o, 1)
    for _ in range(2):
        sum_o.step()
    for _ in range(steps):
        sum_qkv.step()

    qkv_sum = sum_qkv.result()
    grad_w_query = qkv_sum[:, :head_cols]
    kv_sum = qkv_sum[:, head_cols:].reshape(groups, shard_rows // groups, 2 * HEAD_SIZE)
    kv_rel = [lax.dynamic_index_in_dim(kv_sum, b, 0, keepdims=False) for b in blocks]
    kv_in = swap(jnp.stack([kv_rel[1], kv_rel[3]]), "tensor", 4, 1)
    kv_own = kv_rel[0] + kv_in[0]
    kv_other = swap(kv_rel[2] + kv_in[1], "tensor", 4, 2)
    first = kv_head == 0
    kv_low = jnp.where(first, kv_own, kv_other)
    kv_high = jnp.where(first, kv_other, kv_own)
    grad_w_key = jnp.concatenate([kv_low[:, :HEAD_SIZE], kv_high[:, :HEAD_SIZE]], 1)
    grad_w_value = jnp.concatenate([kv_low[:, HEAD_SIZE:], kv_high[:, HEAD_SIZE:]], 1)

    def put(length, vector, index):
        return lax.dynamic_update_slice_in_dim(jnp.zeros((length,), F32), vector, index, 0)

    kv_cols = KEY_VALUE_HEADS * HEAD_SIZE
    packed = jnp.concatenate(
        [
            put(QUERY_HEADS * HEAD_SIZE, grad_qkv_bias[:head_cols], tensor_index * head_cols),
            put(kv_cols, grad_qkv_bias[head_cols : head_cols + HEAD_SIZE], kv_head * HEAD_SIZE),
            put(kv_cols, grad_qkv_bias[head_cols + HEAD_SIZE :], kv_head * HEAD_SIZE),
            grad_gain_one,
            grad_gain_two,
            jnp.full((HEAD_SIZE,), square_sum, F32),
        ]
    )
    packed = sum_small(packed.reshape(-1, HEAD_SIZE), dp_size).reshape(-1)
    device = dp_index * groups + tensor_index
    smalls = []
    at = 0
    for width in (bias_part, kv_part, kv_part, bias_part, bias_part):
        smalls.append(lax.dynamic_slice_in_dim(packed, at + device * width, width, 0))
        at += width * dp_size * groups
    distill_loss = packed[at] / (2.0 * count_all * feature_count)
    return (
        result.astype(BF16),
        distill_loss,
        grad_states,
        grad_w_query,
        grad_w_key,
        grad_w_value,
        sum_o.result().T,
        sum_gate.result(),
        sum_up.result(),
        sum_down.result().T,
        smalls[0],
        smalls[1],
        smalls[2],
        smalls[3],
        smalls[4],
    )


def solution(mesh):
    rows = P(("dp", "tensor"), None)
    flat = P(("dp", "tensor"))
    return jax.shard_map(
        body,
        mesh=mesh,
        in_specs=(
            rows,
            rows,
            rows,
            P("dp"),
            P("dp", None),
            P("dp", "tensor"),
            rows,
            rows,
            P("tensor", "dp"),
            P("dp", "tensor"),
            P("dp", "tensor"),
            P("tensor", "dp"),
            flat,
            flat,
            flat,
            flat,
            flat,
        ),
        out_specs=(
            rows,
            P(),
            rows,
            P("dp", "tensor"),
            rows,
            rows,
            P("tensor", "dp"),
            P("dp", "tensor"),
            P("dp", "tensor"),
            P("tensor", "dp"),
            flat,
            flat,
            flat,
            flat,
            flat,
        ),
        check_vma=False,
    )
```

time: 1590 us -> 1510 us (0.950)
  Pallas kernels: 0 us -> 750 us
  waiting for transfers between devices: 1030 us -> 285 us
  blocking collectives: 211 us -> 0 us
  starting transfers between devices: 11.3 us -> 116 us
  local copies, waits for them, and re-layouts: 34.8 us -> 79.2 us
  matrix products: 208 us -> 179 us
  other arithmetic: 58 us -> 84.6 us
    pallas_call x0 -> x6, Pallas kernels: none -> 750 us  [place(): pl.pallas_call(functools.partial(place_kernel, spans), out_shape=jax.Shap...]
    reduce_scatter x11 -> x0, waiting for transfers between devices: 650 us -> none  [the longest x1 130 us: body(): lax.psum_scatter(grad_down.astype(jnp.bfloat16), 'dp', scatter_dimension=...]
    all_gather x9 -> x0, waiting for transfers between devices: 381 us -> none  [the longest x1 105 us: body(): lax.all_gather(w_gate, 'dp', axis=0, tiled=True)]
    ppermute x0 -> x126, waiting for transfers between devices: none -> 285 us  [the longest x24 80.7 us: step(): self.up = lax.ppermute(up, 'dp', ring_pairs(size, 1))]
    ppermute x0 -> x126, starting transfers between devices: none -> 116 us  [the longest x24 32.3 us: step(): self.up = lax.ppermute(up, 'dp', ring_pairs(size, 1))]
    all_gather x2 -> x0, blocking collectives: 89 us -> none  [the longest x1 45.4 us: body(): lax.all_gather(key_projection_weight, ('dp', 'tensor'), axis=0, tiled=True)]
    psum x2 -> x0, blocking collectives: 78.9 us -> none  [body(): lax.psum((jnp.sum(valid_rows * deviation * deviation), jnp.sum(valid_rows...]
    unnamed x1 -> x0, blocking collectives: 42.7 us -> none
  transfers between devices with their start and end apart: 20 -> 126, of which waited for: 15 -> 52; matrix products, arithmetic and copies ran while one was open for 14% -> 18% of each run, Pallas kernels for 0% -> 36%
where the time goes in v1:
time: 1510 us; the launch traced here: 1500 us
  Pallas kernels  750 us (50%)
  waiting for transfers between devices  285 us (19%)
  matrix products  179 us (12%)
  starting transfers between devices  116 us (8%)
  other arithmetic  84.6 us (6%)
  local copies, waits for them, and re-layouts  79.2 us (5%)
    pallas_call x6, Pallas kernels, place(): pl.pallas_call(functools.partial(place_kernel, spans), out_shape=jax.Shap...  750 us
    dot_general x26, matrix products, mm(): return jnp.einsum(spec, left, right, preferred_element_type=F32)  134 us
    ppermute x24, waiting for transfers between devices, step(): self.up = lax.ppermute(up, 'dp', ring_pairs(size, 1))  80.7 us
    ppermute x20, waiting for transfers between devices, step(): self.down = lax.ppermute(down, 'dp', ring_pairs(self.size, -1))  70.5 us
    ppermute x20, waiting for transfers between devices, step(): self.up = lax.ppermute(up, 'dp', ring_pairs(self.size, 1))  63 us
    ppermute x38, waiting for transfers between devices, swap(): return lax.ppermute(value, axis, [(i, i ^ bits) for i in range(size)])  54.9 us
    ppermute x24, starting transfers between devices, step(): self.up = lax.ppermute(up, 'dp', ring_pairs(size, 1))  32.3 us
  transfers between devices with their start and end apart: 126, of which 52 were waited for; matrix products, arithmetic and copies ran while one was open for 18% of the time, Pallas kernels for 36%

profile of v1, /device:TPU:0, one launch (start us, length us, event | category | flops | bytes accessed | tf_op | source)
XLA Modules:
  0.0 1501.6 jit_solution(9700449852299042591)
XLA Ops:
  52.7 16.6 %collective-permute-done.20.refs_3_ = bf16[192,256]{1,0:T(8,128)(2,1)S(1)} collective-permute-done((bf16[192,256]{1,0:T(8,128)(2,1)S(1)}, bf16[192,256]{1,0:T(8,128)(2,1)S(1)}, u32[]{:S(2)}, u32[]{:S(2)}) %collective-permute-start.20) | collective-permute-done | bytes 98336 | tf_op jit(solution)/shard_map/ppermute | solution.py:80
  97.2 25.7 %shard_map.281 = bf16[8,192,256]{2,1,0:T(8,128)(2,1)} custom-call(s32[9]{0:T(128)} %stack.39.where, bf16[192,256]{1,0:T(8,128)(2,1)} %copy-done.61, bf16[192,256]{1,0:T(8,128)(2,1)} %copy-done.80, bf16[192,256]{1,0:T(8,128)(2,1)} %copy-done.82, bf16[192,256]{1,0:T(8,128)(2,1)} %copy-done.68, bf16[96,256]{1,0:T(8,128)(2,1)} %copy-done.93, ...), custom_call_target="tpu_custom_call" | custom-call | tf_op jit(solution)/shard_map/pallas_call | solution.py:119
  122.9 37.6 %shard_map.280 = bf16[8,192,384]{2,1,0:T(8,128)(2,1)} custom-call(s32[9]{0:T(128)} %stack.39.where, bf16[192,384]{1,0:T(8,128)(2,1)} %refs_0_.3, bf16[192,384]{1,0:T(8,128)(2,1)} %copy-done.70, bf16[192,384]{1,0:T(8,128)(2,1)} %copy-done.74, bf16[192,384]{1,0:T(8,128)(2,1)} %copy-done.62, bf16[96,384]{1,0:T(8,128)(2,1)} %copy-done.87, ...), custom_call_target="tpu_custom_call" | custom-call | tf_op jit(solution)/shard_map/pallas_call | solution.py:119
  160.5 37.6 %shard_map.282 = bf16[8,192,384]{2,1,0:T(8,128)(2,1)} custom-call(s32[9]{0:T(128)} %stack.39.where, bf16[192,384]{1,0:T(8,128)(2,1)} %bitcast.432, bf16[192,384]{1,0:T(8,128)(2,1)} %copy-done.72, bf16[192,384]{1,0:T(8,128)(2,1)} %copy-done.75, bf16[192,384]{1,0:T(8,128)(2,1)} %copy-done.63, bf16[96,384]{1,0:T(8,128)(2,1)} %copy-done.91, ...), custom_call_target="tpu_custom_call" | custom-call | tf_op jit(solution)/shard_map/pallas_call | solution.py:119
  216.5 6.4 fusion.154
  229.7 6.1 fusion.155
  246.9 11.6 collective-permute-done.44.refs_3_
  260.1 6.1 collective-permute-done.45.refs_7_
  272.6 7.9 collective-permute-done.46.refs_4_
  286.7 12.6 collective-permute-done.52.refs_3_
  306.3 20.0 %collective-permute-done.54.refs_4_ = bf16[96,2240]{1,0:T(8,128)(2,1)S(1)} collective-permute-done((bf16[96,2240]{1,0:T(8,128)(2,1)S(1)}, bf16[96,2240]{1,0:T(8,128)(2,1)S(1)}, u32[]{:S(2)}, u32[]{:S(2)}) %collective-permute-start.54) | collective-permute-done | bytes 430112 | tf_op jit(solution)/shard_map/ppermute | solution.py:80
  330.4 216.3 %shard_map.283 = bf16[8,192,2240]{2,1,0:T(8,128)(2,1)} custom-call(s32[9]{0:T(128)} %stack.39.where, bf16[192,2240]{1,0:T(8,128)(2,1)} %refs_0_.4, bf16[192,2240]{1,0:T(8,128)(2,1)} %collective-permute-done.40.refs_1_, bf16[192,2240]{1,0:T(8,128)(2,1)} %collective-permute-done.42.refs_2_, bf16[192,2240]{1,0:T(8,128)(2,1)} %collective-permute-done.44.refs_3_, ...), custom_call_target="tpu_custom_call" | custom-call | tf_op jit(solution)/shard_map/pallas_call | solution.py:119
  546.7 216.3 %shard_map.284 = bf16[8,192,2240]{2,1,0:T(8,128)(2,1)} custom-call(s32[9]{0:T(128)} %stack.39.where, bf16[192,2240]{1,0:T(8,128)(2,1)} %refs_0_.5, bf16[192,2240]{1,0:T(8,128)(2,1)} %collective-permute-done.48.refs_1_, bf16[192,2240]{1,0:T(8,128)(2,1)} %collective-permute-done.50.refs_2_, bf16[192,2240]{1,0:T(8,128)(2,1)} %copy-done.31, ...), custom_call_target="tpu_custom_call" | custom-call | tf_op jit(solution)/shard_map/pallas_call | solution.py:119
  765.1 12.8 fusion.139
  777.9 6.9 collective-permute-done.60.refs_3_
  788.9 17.2 %multiply_convert_fusion.2 = (bf16[1024,2240]{0,1:T(8,128)(2,1)}, f32[1024,2240]{0,1:T(8,128)}) fusion(f32[1024,2240]{0,1:T(8,128)} %fusion.139, bf16[1536,2240]{1,0:T(8,128)(2,1)} %bitcast.381, bf16[256,1536]{1,0:T(8,128)(2,1)} %collective-permute-done.39, bf16[256,1536]{1,0:T(8,128)(2,1)} %collective-permute-done.38, ...), kind=kOutput, calls=%fused_computation.9 | convolution fusion | flops 7072776192 | bytes 32964608 | tf_op jit(solution)/shard_map/dot_general | solution.py:373
  806.1 216.3 %shard_map.285 = bf16[8,192,2240]{2,1,0:T(8,128)(2,1)} custom-call(s32[9]{0:T(128)} %stack.39.where, bf16[192,2240]{1,0:T(8,128)(2,1)} %bitcast.415, bf16[192,2240]{1,0:T(8,128)(2,1)} %collective-permute-done.56.refs_1_, bf16[192,2240]{1,0:T(8,128)(2,1)} %collective-permute-done.58.refs_2_, bf16[192,2240]{1,0:T(8,128)(2,1)} %copy-done.33, ...), custom_call_target="tpu_custom_call" | custom-call | tf_op jit(solution)/shard_map/pallas_call | solution.py:119
  1022.4 7.7 convolution_convert_fusion.4
  1030.3 3.9 convolution_convert_fusion.5
  1037.3 18.1 %collective-permute-done.66 = bf16[256,1536]{1,0:T(8,128)(2,1)} collective-permute-done((bf16[256,1536]{1,0:T(8,128)(2,1)S(1)}, bf16[256,1536]{1,0:T(8,128)(2,1)}, u32[]{:S(2)}, u32[]{:S(2)}) %collective-permute-start.66) | collective-permute-done | bytes 786464 | tf_op jit(solution)/shard_map/ppermute | solution.py:47
  1060.2 18.8 %collective-permute-done.68 = bf16[256,1536]{1,0:T(8,128)(2,1)} collective-permute-done((bf16[256,1536]{1,0:T(8,128)(2,1)}, bf16[256,1536]{1,0:T(8,128)(2,1)}, u32[]{:S(2)}, u32[]{:S(2)}) %collective-permute-start.68) | collective-permute-done | bytes 786464 | tf_op jit(solution)/shard_map/ppermute | solution.py:47
  1083.7 18.9 %multiply_convert_fusion.1 = (bf16[1024,2240]{0,1:T(8,128)(2,1)}, bf16[1024,2240]{0,1:T(8,128)(2,1)}) fusion(f32[1024,2240]{0,1:T(8,128)} %fusion.139, f32[1024,2240]{0,1:T(8,128)} %get-tuple-element.223, bf16[1536,2240]{1,0:T(8,128)(2,1)} %bitcast.385, bf16[256,1536]{1,0:T(8,128)(2,1)} %collective-permute-done.69, ...), kind=kOutput, calls=%fused_computation.8 | convolution fusion | flops 7088832512 | bytes 37552128 | tf_op jit(solution)/shard_map/rd,df->rf/dot_general | solution.py:23
  1102.6 7.2 fusion.18
  1109.8 8.7 fusion.21
  1118.6 3.9 fusion.17
  1124.4 5.9 fusion.16
  1132.8 11.6 convolution_convert_fusion
  1144.5 9.8 copy.135
  1159.0 12.3 convolution_convert_fusion.2
  1171.3 11.1 convolution_convert_fusion.1
  1182.4 9.7 copy.133
  1192.1 9.8 copy.134
  1210.5 15.6 %collective-permute-done.95 = bf16[192,2240]{1,0:T(8,128)(2,1)S(1)} collective-permute-done((bf16[192,2240]{1,0:T(8,128)(2,1)S(1)}, bf16[192,2240]{1,0:T(8,128)(2,1)S(1)}, u32[]{:S(2)}, u32[]{:S(2)}) %collective-permute-start.95) | collective-permute-done | bytes 860192 | tf_op jit(solution)/shard_map/ppermute | solution.py:155
  1244.8 14.3 collective-permute-done.115
  1265.8 13.4 collective-permute-done.100
  1283.1 12.4 collective-permute-done.116
  1300.7 5.9 collective-permute-done.103
  1312.8 4.4 convolution_convert_fusion.9
  1318.6 4.8 fusion.5
  1323.4 4.8 fusion.2
  1328.1 4.6 fusion.4
  1336.5 4.6 fusion.7
  1347.5 7.1 fusion.142
  1395.0 10.4 collective-permute-done.118
  1420.0 14.1 collective-permute-done.91
  1442.3 4.4 collective-permute-done.112
  1461.3 14.7 collective-permute-done.123
  1484.5 12.2 collective-permute-done.125
  (695 shorter events, 314.7 us)
Async XLA Ops:
  0.6 34.9 %collective-permute-start.8 = (bf16[192,384]{1,0:T(8,128)(2,1)}, bf16[192,384]{1,0:T(8,128)(2,1)S(1)}, u32[]{:S(2)}, u32[]{:S(2)}) collective-permute-start(bf16[192,384]{1,0:T(8,128)(2,1)} %refs_0_.3), channel_id=1, source_target_pairs={{0,8},{8,16},{16,24},{24,28},{28,20},{20,12},{12,4},{4,0},{1,9},{9... | collective-permute-start | bytes 442376 | tf_op jit(solution)/shard_map/ppermute | solution.py:80
  3.7 32.5 %collective-permute-start.12 = (bf16[192,384]{1,0:T(8,128)(2,1)}, bf16[192,384]{1,0:T(8,128)(2,1)S(1)}, u32[]{:S(2)}, u32[]{:S(2)}) collective-permute-start(bf16[192,384]{1,0:T(8,128)(2,1)} %refs_0_.3), channel_id=1, source_target_pairs={{0,4},{8,0},{16,8},{24,16},{28,24},{20,28},{12,20},{4,12},{1,5},{9... | collective-permute-start | bytes 442376 | tf_op jit(solution)/shard_map/ppermute | solution.py:81
  14.2 23.5 %collective-permute-start.26 = (bf16[192,384]{1,0:T(8,128)(2,1)}, bf16[192,384]{1,0:T(8,128)(2,1)S(1)}, u32[]{:S(2)}, u32[]{:S(2)}) collective-permute-start(bf16[192,384]{1,0:T(8,128)(2,1)} %bitcast.430), channel_id=1, source_target_pairs={{0,8},{8,16},{16,24},{24,28},{28,20},{20,12},{12,4},{4,0},{1,9},{9... | collective-permute-start | bytes 442376 | tf_op jit(solution)/shard_map/ppermute | solution.py:80
  45.4 44.8 %collective-permute-start.40 = (bf16[192,2240]{1,0:T(8,128)(2,1)}, bf16[192,2240]{1,0:T(8,128)(2,1)}, u32[]{:S(2)}, u32[]{:S(2)}) collective-permute-start(bf16[192,2240]{1,0:T(8,128)(2,1)} %refs_0_.4), channel_id=1, source_target_pairs={{0,8},{8,16},{16,24},{24,28},{28,20},{20,12},{12,4},{4,0},{1,9},{9... | collective-permute-start | bytes 2580488 | tf_op jit(solution)/shard_map/ppermute | solution.py:80
  52.1 37.9 %collective-permute-start.1 = (bf16[256,1536]{1,0:T(8,128)(2,1)}, bf16[256,1536]{1,0:T(8,128)(2,1)S(1)}, u32[]{:S(2)}, u32[]{:S(2)}) collective-permute-start(bf16[256,1536]{1,0:T(8,128)(2,1)} %param.17), channel_id=1, source_target_pairs={{0,2},{1,3},{2,0},{3,1},{4,6},{5,7},{6,4},{7,5},{8,10},{9,11},{10,... | collective-permute-start | bytes 2359304 | tf_op jit(solution)/shard_map/ppermute | solution.py:47
  85.0 113.1 %collective-permute-start.41 = (bf16[192,2240]{1,0:T(8,128)(2,1)}, bf16[192,2240]{1,0:T(8,128)(2,1)}, u32[]{:S(2)}, u32[]{:S(2)}) collective-permute-start(bf16[192,2240]{1,0:T(8,128)(2,1)} %refs_0_.4), channel_id=1, source_target_pairs={{0,4},{8,0},{16,8},{24,16},{28,24},{20,28},{12,20},{4,12},{1,5},{9... | collective-permute-start | bytes 2580488 | tf_op jit(solution)/shard_map/ppermute | solution.py:81
  86.8 112.8 %collective-permute-start.48 = (bf16[192,2240]{1,0:T(8,128)(2,1)}, bf16[192,2240]{1,0:T(8,128)(2,1)}, u32[]{:S(2)}, u32[]{:S(2)}) collective-permute-start(bf16[192,2240]{1,0:T(8,128)(2,1)} %refs_0_.5), channel_id=1, source_target_pairs={{0,8},{8,16},{16,24},{24,28},{28,20},{20,12},{12,4},{4,0},{1,9},{9... | collective-permute-start | bytes 2580488 | tf_op jit(solution)/shard_map/ppermute | solution.py:80
  88.2 112.0 %collective-permute-start.49 = (bf16[192,2240]{1,0:T(8,128)(2,1)}, bf16[192,2240]{1,0:T(8,128)(2,1)}, u32[]{:S(2)}, u32[]{:S(2)}) collective-permute-start(bf16[192,2240]{1,0:T(8,128)(2,1)} %refs_0_.5), channel_id=1, source_target_pairs={{0,4},{8,0},{16,8},{24,16},{28,24},{20,28},{12,20},{4,12},{1,5},{9... | collective-permute-start | bytes 2580488 | tf_op jit(solution)/shard_map/ppermute | solution.py:81
  90.0 111.6 %collective-permute-start = (bf16[256,1536]{1,0:T(8,128)(2,1)S(1)}, bf16[256,1536]{1,0:T(8,128)(2,1)S(1)}, u32[]{:S(2)}, u32[]{:S(2)}) collective-permute-start(bf16[256,1536]{1,0:T(8,128)(2,1)S(1)} %copy-done.18), channel_id=1, source_target_pairs={{0,1},{1,0},{2,3},{3,2},{4,5},{5,4},{6,7},{7,6},{8,9},{9,8},{10,11... | collective-permute-start | bytes 2359304 | tf_op jit(solution)/shard_map/ppermute | solution.py:47
  90.2 112.1 %collective-permute-start.2 = (bf16[256,1536]{1,0:T(8,128)(2,1)S(1)}, bf16[256,1536]{1,0:T(8,128)(2,1)S(1)}, u32[]{:S(2)}, u32[]{:S(2)}) collective-permute-start(bf16[256,1536]{1,0:T(8,128)(2,1)S(1)} %collective-permute-done.1), channel_id=1, source_target_pairs={{0,1},{1,0},{2,3},{3,2},{4,5},{5,4},{6,7},{7,6},{8,9},{9,8},{10,11... | collective-permute-start | bytes 2359304 | tf_op jit(solution)/shard_map/ppermute | solution.py:47
  198.1 37.8 %collective-permute-start.42 = (bf16[192,2240]{1,0:T(8,128)(2,1)}, bf16[192,2240]{1,0:T(8,128)(2,1)}, u32[]{:S(2)}, u32[]{:S(2)}) collective-permute-start(bf16[192,2240]{1,0:T(8,128)(2,1)} %collective-permute-done.40.refs_1_), channel_id=1, source_target_pairs={{0,8},{8,16},{16,24},{24,28},{28,20},{20,12},{12,4},{4,0},{1,9},{9... | collective-permute-start | bytes 2580488 | tf_op jit(solution)/shard_map/ppermute | solution.py:80
  199.6 36.3 %collective-permute-start.43 = (bf16[192,2240]{1,0:T(8,128)(2,1)}, bf16[192,2240]{1,0:T(8,128)(2,1)}, u32[]{:S(2)}, u32[]{:S(2)}) collective-permute-start(bf16[192,2240]{1,0:T(8,128)(2,1)} %collective-permute-done.41.refs_5_), channel_id=1, source_target_pairs={{0,4},{8,0},{16,8},{24,16},{28,24},{20,28},{12,20},{4,12},{1,5},{9... | collective-permute-start | bytes 2580488 | tf_op jit(solution)/shard_map/ppermute | solution.py:81
  200.2 68.3 %collective-permute-start.50 = (bf16[192,2240]{1,0:T(8,128)(2,1)}, bf16[192,2240]{1,0:T(8,128)(2,1)}, u32[]{:S(2)}, u32[]{:S(2)}) collective-permute-start(bf16[192,2240]{1,0:T(8,128)(2,1)} %collective-permute-done.48.refs_1_), channel_id=1, source_target_pairs={{0,8},{8,16},{16,24},{24,28},{28,20},{20,12},{12,4},{4,0},{1,9},{9... | collective-permute-start | bytes 2580488 | tf_op jit(solution)/shard_map/ppermute | solution.py:80
  201.6 69.8 %collective-permute-start.51 = (bf16[192,2240]{1,0:T(8,128)(2,1)}, bf16[192,2240]{1,0:T(8,128)(2,1)}, u32[]{:S(2)}, u32[]{:S(2)}) collective-permute-start(bf16[192,2240]{1,0:T(8,128)(2,1)} %collective-permute-done.49.refs_5_), channel_id=1, source_target_pairs={{0,4},{8,0},{16,8},{24,16},{28,24},{20,28},{12,20},{4,12},{1,5},{9... | collective-permute-start | bytes 2580488 | tf_op jit(solution)/shard_map/ppermute | solution.py:81
  243.9 38.7 %collective-permute-start.34 = (bf16[256,1536]{1,0:T(8,128)(2,1)}, bf16[256,1536]{1,0:T(8,128)(2,1)}, u32[]{:S(2)}, u32[]{:S(2)}) collective-permute-start(bf16[256,1536]{1,0:T(8,128)(2,1)} %slice.562), channel_id=1, source_target_pairs={{0,1},{1,0},{2,3},{3,2},{4,5},{5,4},{6,7},{7,6},{8,9},{9,8},{10,11... | collective-permute-start | bytes 2359304 | tf_op jit(solution)/shard_map/ppermute | solution.py:47
  258.5 24.7 %collective-permute-start.36 = (bf16[256,1536]{1,0:T(8,128)(2,1)}, bf16[256,1536]{1,0:T(8,128)(2,1)}, u32[]{:S(2)}, u32[]{:S(2)}) collective-permute-start(bf16[256,1536]{1,0:T(8,128)(2,1)} %add_convert_fusion.4), channel_id=1, source_target_pairs={{0,2},{1,3},{2,0},{3,1},{4,6},{5,7},{6,4},{7,5},{8,10},{9,11},{10,... | collective-permute-start | bytes 2359304 | tf_op jit(solution)/shard_map/ppermute | solution.py:47
  271.4 27.9 %collective-permute-start.52 = (bf16[192,2240]{1,0:T(8,128)(2,1)}, bf16[192,2240]{1,0:T(8,128)(2,1)S(1)}, u32[]{:S(2)}, u32[]{:S(2)}) collective-permute-start(bf16[192,2240]{1,0:T(8,128)(2,1)} %collective-permute-done.50.refs_2_), channel_id=1, source_target_pairs={{0,8},{8,16},{16,24},{24,28},{28,20},{20,12},{12,4},{4,0},{1,9},{9... | collective-permute-start | bytes 2580488 | tf_op jit(solution)/shard_map/ppermute | solution.py:80
  281.1 46.7 %collective-permute-start.56 = (bf16[192,2240]{1,0:T(8,128)(2,1)S(1)}, bf16[192,2240]{1,0:T(8,128)(2,1)}, u32[]{:S(2)}, u32[]{:S(2)}) collective-permute-start(bf16[192,2240]{1,0:T(8,128)(2,1)S(1)} %bitcast.416), channel_id=1, source_target_pairs={{0,8},{8,16},{16,24},{24,28},{28,20},{20,12},{12,4},{4,0},{1,9},{9... | collective-permute-start | bytes 2580488 | tf_op jit(solution)/shard_map/ppermute | solution.py:80
  282.6 45.2 %collective-permute-start.57 = (bf16[192,2240]{1,0:T(8,128)(2,1)S(1)}, bf16[192,2240]{1,0:T(8,128)(2,1)}, u32[]{:S(2)}, u32[]{:S(2)}) collective-permute-start(bf16[192,2240]{1,0:T(8,128)(2,1)S(1)} %bitcast.417), channel_id=1, source_target_pairs={{0,4},{8,0},{16,8},{24,16},{28,24},{20,28},{12,20},{4,12},{1,5},{9... | collective-permute-start | bytes 2580488 | tf_op jit(solution)/shard_map/ppermute | solution.py:81
  286.2 43.7 %collective-permute-start.38 = (bf16[256,1536]{1,0:T(8,128)(2,1)}, bf16[256,1536]{1,0:T(8,128)(2,1)}, u32[]{:S(2)}, u32[]{:S(2)}) collective-permute-start(bf16[256,1536]{1,0:T(8,128)(2,1)} %multiply_convert_fusion.4), channel_id=1, source_target_pairs={{0,2},{1,3},{2,0},{3,1},{4,6},{5,7},{6,4},{7,5},{8,10},{9,11},{10,... | collective-permute-start | bytes 2359304 | tf_op jit(solution)/shard_map/ppermute | solution.py:47
  327.8 435.1 %collective-permute-start.58 = (bf16[192,2240]{1,0:T(8,128)(2,1)}, bf16[192,2240]{1,0:T(8,128)(2,1)}, u32[]{:S(2)}, u32[]{:S(2)}) collective-permute-start(bf16[192,2240]{1,0:T(8,128)(2,1)} %collective-permute-done.56.refs_1_), channel_id=1, source_target_pairs={{0,8},{8,16},{16,24},{24,28},{28,20},{20,12},{12,4},{4,0},{1,9},{9... | collective-permute-start | bytes 2580488 | tf_op jit(solution)/shard_map/ppermute | solution.py:80
  329.0 434.0 %collective-permute-start.59 = (bf16[192,2240]{1,0:T(8,128)(2,1)}, bf16[192,2240]{1,0:T(8,128)(2,1)}, u32[]{:S(2)}, u32[]{:S(2)}) collective-permute-start(bf16[192,2240]{1,0:T(8,128)(2,1)} %collective-permute-done.57.refs_5_), channel_id=1, source_target_pairs={{0,4},{8,0},{16,8},{24,16},{28,24},{20,28},{12,20},{4,12},{1,5},{9... | collective-permute-start | bytes 2580488 | tf_op jit(solution)/shard_map/ppermute | solution.py:81
  329.9 435.2 %collective-permute-start.37 = (bf16[256,1536]{1,0:T(8,128)(2,1)}, bf16[256,1536]{1,0:T(8,128)(2,1)}, u32[]{:S(2)}, u32[]{:S(2)}) collective-permute-start(bf16[256,1536]{1,0:T(8,128)(2,1)} %multiply_convert_fusion.4), channel_id=1, source_target_pairs={{0,1},{1,0},{2,3},{3,2},{4,5},{5,4},{6,7},{7,6},{8,9},{9,8},{10,11... | collective-permute-start | bytes 2359304 | tf_op jit(solution)/shard_map/ppermute | solution.py:47
  329.9 435.2 %collective-permute-start.39 = (bf16[256,1536]{1,0:T(8,128)(2,1)}, bf16[256,1536]{1,0:T(8,128)(2,1)}, u32[]{:S(2)}, u32[]{:S(2)}) collective-permute-start(bf16[256,1536]{1,0:T(8,128)(2,1)} %collective-permute-done.38), channel_id=1, source_target_pairs={{0,1},{1,0},{2,3},{3,2},{4,5},{5,4},{6,7},{7,6},{8,9},{9,8},{10,11... | collective-permute-start | bytes 2359304 | tf_op jit(solution)/shard_map/ppermute | solution.py:47
  1060.2 23.5 %collective-permute-start.67 = (bf16[256,1536]{1,0:T(8,128)(2,1)}, bf16[256,1536]{1,0:T(8,128)(2,1)}, u32[]{:S(2)}, u32[]{:S(2)}) collective-permute-start(bf16[256,1536]{1,0:T(8,128)(2,1)} %fusion.117), channel_id=1, source_target_pairs={{0,1},{1,0},{2,3},{3,2},{4,5},{5,4},{6,7},{7,6},{8,9},{9,8},{10,11... | collective-permute-start | bytes 2359304 | tf_op jit(solution)/shard_map/ppermute | solution.py:47
  1123.9 84.6 %collective-permute-start.71 = (bf16[256,1536]{1,0:T(8,128)(2,1)}, bf16[256,1536]{1,0:T(8,128)(2,1)}, u32[]{:S(2)}, u32[]{:S(2)}) collective-permute-start(bf16[256,1536]{1,0:T(8,128)(2,1)} %slice.587), channel_id=1, source_target_pairs={{0,1},{1,0},{2,3},{3,2},{4,5},{5,4},{6,7},{7,6},{8,9},{9,8},{10,11... | collective-permute-start | bytes 2359304 | tf_op jit(solution)/shard_map/ppermute | solution.py:47
  1132.4 99.8 %collective-permute-start.70 = (bf16[256,1536]{1,0:T(8,128)(2,1)}, bf16[256,1536]{1,0:T(8,128)(2,1)}, u32[]{:S(2)}, u32[]{:S(2)}) collective-permute-start(bf16[256,1536]{1,0:T(8,128)(2,1)} %slice.583), channel_id=1, source_target_pairs={{0,1},{1,0},{2,3},{3,2},{4,5},{5,4},{6,7},{7,6},{8,9},{9,8},{10,11... | collective-permute-start | bytes 2359304 | tf_op jit(solution)/shard_map/ppermute | solution.py:47
  1156.9 45.0 %collective-permute-start.96 = (bf16[96,2240]{1,0:T(8,128)(2,1)}, bf16[96,2240]{1,0:T(8,128)(2,1)}, u32[]{:S(2)}, u32[]{:S(2)}) collective-permute-start(bf16[96,2240]{1,0:T(8,128)(2,1)} %get-tuple-element.145), channel_id=1, source_target_pairs={{0,4},{8,0},{16,8},{24,16},{28,24},{20,28},{12,20},{4,12},{1,5},{9... | collective-permute-start | bytes 1290248 | tf_op jit(solution)/shard_map/ppermute | solution.py:156
  1157.8 44.1 %collective-permute-start.94 = (bf16[96,2240]{1,0:T(8,128)(2,1)}, bf16[96,2240]{1,0:T(8,128)(2,1)}, u32[]{:S(2)}, u32[]{:S(2)}) collective-permute-start(bf16[96,2240]{1,0:T(8,128)(2,1)} %get-tuple-element.144), channel_id=1, source_target_pairs={{0,8},{8,16},{16,24},{24,28},{28,20},{20,12},{12,4},{4,0},{1,9},{9... | collective-permute-start | bytes 1290248 | tf_op jit(solution)/shard_map/ppermute | solution.py:155
  1209.9 23.4 %collective-permute-start.72 = (bf16[256,1536]{1,0:T(8,128)(2,1)S(1)}, bf16[256,1536]{1,0:T(8,128)(2,1)S(1)}, u32[]{:S(2)}, u32[]{:S(2)}) collective-permute-start(bf16[256,1536]{1,0:T(8,128)(2,1)S(1)} %add_convert_fusion.2), channel_id=1, source_target_pairs={{0,2},{1,3},{2,0},{3,1},{4,6},{5,7},{6,4},{7,5},{8,10},{9,11},{10,... | collective-permute-start | bytes 2359304 | tf_op jit(solution)/shard_map/ppermute | solution.py:47
  1231.2 27.9 %collective-permute-start.115 = (bf16[192,2240]{1,0:T(8,128)(2,1)S(1)}, bf16[192,2240]{1,0:T(8,128)(2,1)S(1)}, u32[]{:S(2)}, u32[]{:S(2)}) collective-permute-start(bf16[192,2240]{1,0:T(8,128)(2,1)S(1)} %get-tuple-element.96), channel_id=1, source_target_pairs={{0,4},{8,0},{16,8},{24,16},{28,24},{20,28},{12,20},{4,12},{1,5},{9... | collective-permute-start | bytes 2580488 | tf_op jit(solution)/shard_map/ppermute | solution.py:156
  1232.2 28.0 %collective-permute-start.114 = (bf16[192,2240]{1,0:T(8,128)(2,1)S(1)}, bf16[192,2240]{1,0:T(8,128)(2,1)S(1)}, u32[]{:S(2)}, u32[]{:S(2)}) collective-permute-start(bf16[192,2240]{1,0:T(8,128)(2,1)S(1)} %get-tuple-element.95), channel_id=1, source_target_pairs={{0,8},{8,16},{16,24},{24,28},{28,20},{20,12},{12,4},{4,0},{1,9},{9... | collective-permute-start | bytes 2580488 | tf_op jit(solution)/shard_map/ppermute | solution.py:155
  1238.7 27.0 %collective-permute-start.74 = (bf16[256,1536]{1,0:T(8,128)(2,1)S(1)}, bf16[256,1536]{1,0:T(8,128)(2,1)S(1)}, u32[]{:S(2)}, u32[]{:S(2)}) collective-permute-start(bf16[256,1536]{1,0:T(8,128)(2,1)S(1)} %get-tuple-element.113), channel_id=1, source_target_pairs={{0,2},{1,3},{2,0},{3,1},{4,6},{5,7},{6,4},{7,5},{8,10},{9,11},{10,... | collective-permute-start | bytes 2359304 | tf_op jit(solution)/shard_map/ppermute | solution.py:47
  1242.8 36.4 %collective-permute-start.100 = (bf16[192,2240]{1,0:T(8,128)(2,1)S(1)}, bf16[192,2240]{1,0:T(8,128)(2,1)S(1)}, u32[]{:S(2)}, u32[]{:S(2)}) collective-permute-start(bf16[192,2240]{1,0:T(8,128)(2,1)S(1)} %pad_maximum_fusion.10), channel_id=1, source_target_pairs={{0,8},{8,16},{16,24},{24,28},{28,20},{20,12},{12,4},{4,0},{1,9},{9... | collective-permute-start | bytes 2580488 | tf_op jit(solution)/shard_map/ppermute | solution.py:155
  1243.9 35.2 %collective-permute-start.101 = (bf16[192,2240]{1,0:T(8,128)(2,1)S(1)}, bf16[192,2240]{1,0:T(8,128)(2,1)S(1)}, u32[]{:S(2)}, u32[]{:S(2)}) collective-permute-start(bf16[192,2240]{1,0:T(8,128)(2,1)S(1)} %pad_maximum_fusion.11), channel_id=1, source_target_pairs={{0,4},{8,0},{16,8},{24,16},{28,24},{20,28},{12,20},{4,12},{1,5},{9... | collective-permute-start | bytes 2580488 | tf_op jit(solution)/shard_map/ppermute | solution.py:156
  1262.1 33.4 %collective-permute-start.116 = (bf16[192,2240]{1,0:T(8,128)(2,1)S(1)}, bf16[192,2240]{1,0:T(8,128)(2,1)S(1)}, u32[]{:S(2)}, u32[]{:S(2)}) collective-permute-start(bf16[192,2240]{1,0:T(8,128)(2,1)S(1)} %get-tuple-element.97), channel_id=1, source_target_pairs={{0,8},{8,16},{16,24},{24,28},{28,20},{20,12},{12,4},{4,0},{1,9},{9... | collective-permute-start | bytes 2580488 | tf_op jit(solution)/shard_map/ppermute | solution.py:155
  1263.3 33.8 %collective-permute-start.117 = (bf16[192,2240]{1,0:T(8,128)(2,1)S(1)}, bf16[192,2240]{1,0:T(8,128)(2,1)S(1)}, u32[]{:S(2)}, u32[]{:S(2)}) collective-permute-start(bf16[192,2240]{1,0:T(8,128)(2,1)S(1)} %get-tuple-element.98), channel_id=1, source_target_pairs={{0,4},{8,0},{16,8},{24,16},{28,24},{20,28},{12,20},{4,12},{1,5},{9... | collective-permute-start | bytes 2580488 | tf_op jit(solution)/shard_map/ppermute | solution.py:156
  1265.7 46.2 %collective-permute-start.73 = (bf16[256,1536]{1,0:T(8,128)(2,1)S(1)}, bf16[256,1536]{1,0:T(8,128)(2,1)S(1)}, u32[]{:S(2)}, u32[]{:S(2)}) collective-permute-start(bf16[256,1536]{1,0:T(8,128)(2,1)S(1)} %get-tuple-element.113), channel_id=1, source_target_pairs={{0,1},{1,0},{2,3},{3,2},{4,5},{5,4},{6,7},{7,6},{8,9},{9,8},{10,11... | collective-permute-start | bytes 2359304 | tf_op jit(solution)/shard_map/ppermute | solution.py:47
  1279.2 32.8 %collective-permute-start.75 = (bf16[256,1536]{1,0:T(8,128)(2,1)S(1)}, bf16[256,1536]{1,0:T(8,128)(2,1)S(1)}, u32[]{:S(2)}, u32[]{:S(2)}) collective-permute-start(bf16[256,1536]{1,0:T(8,128)(2,1)S(1)} %collective-permute-done.74), channel_id=1, source_target_pairs={{0,1},{1,0},{2,3},{3,2},{4,5},{5,4},{6,7},{7,6},{8,9},{9,8},{10,11... | collective-permute-start | bytes 2359304 | tf_op jit(solution)/shard_map/ppermute | solution.py:47
  1279.2 27.4 %collective-permute-start.103 = (bf16[96,2240]{1,0:T(8,128)(2,1)S(1)}, bf16[96,2240]{1,0:T(8,128)(2,1)S(1)}, u32[]{:S(2)}, u32[]{:S(2)}) collective-permute-start(bf16[96,2240]{1,0:T(8,128)(2,1)S(1)} %get-tuple-element.88), channel_id=1, source_target_pairs={{0,4},{8,0},{16,8},{24,16},{28,24},{20,28},{12,20},{4,12},{1,5},{9... | collective-permute-start | bytes 1290248 | tf_op jit(solution)/shard_map/ppermute | solution.py:156
  1297.1 97.8 %collective-permute-start.119 = (bf16[192,2240]{1,0:T(8,128)(2,1)}, bf16[192,2240]{1,0:T(8,128)(2,1)}, u32[]{:S(2)}, u32[]{:S(2)}) collective-permute-start(bf16[192,2240]{1,0:T(8,128)(2,1)} %get-tuple-element.100), channel_id=1, source_target_pairs={{0,4},{8,0},{16,8},{24,16},{28,24},{20,28},{12,20},{4,12},{1,5},{9... | collective-permute-start | bytes 2580488 | tf_op jit(solution)/shard_map/ppermute | solution.py:156
  1309.9 79.5 %collective-permute-start.104 = (bf16[192,2240]{1,0:T(8,128)(2,1)}, bf16[192,2240]{1,0:T(8,128)(2,1)}, u32[]{:S(2)}, u32[]{:S(2)}) collective-permute-start(bf16[192,2240]{1,0:T(8,128)(2,1)} %pad_maximum_fusion.12), channel_id=1, source_target_pairs={{0,8},{8,16},{16,24},{24,28},{28,20},{20,12},{12,4},{4,0},{1,9},{9... | collective-permute-start | bytes 2580488 | tf_op jit(solution)/shard_map/ppermute | solution.py:155
  1310.5 79.5 %collective-permute-start.105 = (bf16[192,2240]{1,0:T(8,128)(2,1)}, bf16[192,2240]{1,0:T(8,128)(2,1)}, u32[]{:S(2)}, u32[]{:S(2)}) collective-permute-start(bf16[192,2240]{1,0:T(8,128)(2,1)} %pad_maximum_fusion.13), channel_id=1, source_target_pairs={{0,4},{8,0},{16,8},{24,16},{28,24},{20,28},{12,20},{4,12},{1,5},{9... | collective-permute-start | bytes 2580488 | tf_op jit(solution)/shard_map/ppermute | solution.py:156
  1388.1 25.6 %collective-permute-start.82 = (bf16[256,1536]{1,0:T(8,128)(2,1)}, bf16[256,1536]{1,0:T(8,128)(2,1)S(1)}, u32[]{:S(2)}, u32[]{:S(2)}) collective-permute-start(bf16[256,1536]{1,0:T(8,128)(2,1)} %get-tuple-element.155), channel_id=1, source_target_pairs={{0,1},{1,0},{2,3},{3,2},{4,5},{5,4},{6,7},{7,6},{8,9},{9,8},{10,11... | collective-permute-start | bytes 2359304 | tf_op jit(solution)/shard_map/ppermute | solution.py:47
  1389.4 71.3 %collective-permute-start.81 = (bf16[256,1536]{1,0:T(8,128)(2,1)}, bf16[256,1536]{1,0:T(8,128)(2,1)S(1)}, u32[]{:S(2)}, u32[]{:S(2)}) collective-permute-start(bf16[256,1536]{1,0:T(8,128)(2,1)} %get-tuple-element.154), channel_id=1, source_target_pairs={{0,1},{1,0},{2,3},{3,2},{4,5},{5,4},{6,7},{7,6},{8,9},{9,8},{10,11... | collective-permute-start | bytes 2359304 | tf_op jit(solution)/shard_map/ppermute | solution.py:47
  1410.5 42.7 %collective-permute-start.121 = (bf16[192,2240]{1,0:T(8,128)(2,1)S(1)}, bf16[192,2240]{1,0:T(8,128)(2,1)S(1)}, u32[]{:S(2)}, u32[]{:S(2)}) collective-permute-start(bf16[192,2240]{1,0:T(8,128)(2,1)S(1)} %get-tuple-element.102), channel_id=1, source_target_pairs={{0,4},{8,0},{16,8},{24,16},{28,24},{20,28},{12,20},{4,12},{1,5},{9... | collective-permute-start | bytes 2580488 | tf_op jit(solution)/shard_map/ppermute | solution.py:156
  1417.8 36.9 %collective-permute-start.120 = (bf16[192,2240]{1,0:T(8,128)(2,1)S(1)}, bf16[192,2240]{1,0:T(8,128)(2,1)S(1)}, u32[]{:S(2)}, u32[]{:S(2)}) collective-permute-start(bf16[192,2240]{1,0:T(8,128)(2,1)S(1)} %get-tuple-element.101), channel_id=1, source_target_pairs={{0,8},{8,16},{16,24},{24,28},{28,20},{20,12},{12,4},{4,0},{1,9},{9... | collective-permute-start | bytes 2580488 | tf_op jit(solution)/shard_map/ppermute | solution.py:155
  1437.2 23.6 %collective-permute-start.83 = (bf16[256,1536]{1,0:T(8,128)(2,1)S(1)}, bf16[256,1536]{1,0:T(8,128)(2,1)S(1)}, u32[]{:S(2)}, u32[]{:S(2)}) collective-permute-start(bf16[256,1536]{1,0:T(8,128)(2,1)S(1)} %add_convert_fusion), channel_id=1, source_target_pairs={{0,2},{1,3},{2,0},{3,1},{4,6},{5,7},{6,4},{7,5},{8,10},{9,11},{10,... | collective-permute-start | bytes 2359304 | tf_op jit(solution)/shard_map/ppermute | solution.py:47
  (210 other events, 4076.3 us)

commit v2 on v1

--- a/solution.py
+++ b/solution.py
@@ -5,6 +5,7 @@
 from jax import lax
 from jax.experimental import pallas as pl
 from jax.experimental.pallas import tpu as pltpu
+from jax.experimental.layout import Layout, with_layout_constraint
 from jax.sharding import PartitionSpec as P
 
 QUERY_HEADS = 12
@@ -41,6 +42,24 @@
 
 def after(value, *tokens):
     return lax.optimization_barrier((value,) + tokens)[0]
+
+
+class Line:
+    def __init__(self):
+        self.last = ()
+
+    def hold(self, *values):
+        if self.last:
+            values = lax.optimization_barrier(tuple(values) + tuple(self.last))[: len(values)]
+        return values if len(values) > 1 else values[0]
+
+    def mark(self, *tokens):
+        self.last = tokens
+
+    def pass_by(self, *values):
+        values = self.hold(*values)
+        self.last = values if isinstance(values, tuple) else (values,)
+        return values
 
 
 def swap(value, axis, size, bits):
@@ -70,13 +89,12 @@
         self.steps = size // 2
         self.done = 0
 
-    def step(self, *tokens):
+    def step(self, line):
         size, rows = self.size, self.shard.shape[0]
         up, down = self.up, self.down
         if self.done == self.steps - 1:
             up, down = up[: rows // 2], down[rows // 2 :]
-        if tokens:
-            up, down = lax.optimization_barrier((up, down) + tokens)[:2]
+        up, down = line.pass_by(up, down)
         self.up = lax.ppermute(up, "dp", ring_pairs(size, 1))
         self.down = lax.ppermute(down, "dp", ring_pairs(size, -1))
         self.ups.append(self.up)
@@ -99,29 +117,38 @@
 
 
 def place_kernel(spans, where, *refs):
-    blocks, (out, sem) = refs[: len(spans)], refs[len(spans) :]
-    copies = []
+    count = len(spans)
+    blocks, out = refs[:count], refs[count]
+    held, sem_in, sem_out = refs[count + 1 :]
+    loads, stores = [], []
     for k, (start, length) in enumerate(spans):
-        copies.append(
-            pltpu.make_async_copy(
-                blocks[k], out.at[where[k], pl.ds(start, length)], sem.at[k]
-            )
-        )
-    for copy in copies:
+        part = held.at[k, pl.ds(0, length)]
+        loads.append(pltpu.make_async_copy(blocks[k], part, sem_in.at[k]))
+        target = out.at[where[k], pl.ds(start, length)]
+        stores.append(pltpu.make_async_copy(part, target, sem_out.at[k]))
+    for copy in loads:
         copy.start()
-    for copy in copies:
+    for load, store in zip(loads, stores):
+        load.wait()
+        store.start()
+    for copy in stores:
         copy.wait()
 
 
 def place(blocks, spans, where, size):
     rows, cols = blocks[0].shape
+    count = len(blocks)
     anywhere = pl.BlockSpec(memory_space=pl.ANY)
     return pl.pallas_call(
         functools.partial(place_kernel, spans),
         out_shape=jax.ShapeDtypeStruct((size, rows, cols), blocks[0].dtype),
-        in_specs=[pl.BlockSpec(memory_space=pltpu.SMEM)] + [anywhere] * len(blocks),
+        in_specs=[pl.BlockSpec(memory_space=pltpu.SMEM)] + [anywhere] * count,
         out_specs=anywhere,
-        scratch_shapes=[pltpu.SemaphoreType.DMA((len(blocks),))],
+        scratch_shapes=[
+            pltpu.VMEM((count, rows, cols), blocks[0].dtype),
+            pltpu.SemaphoreType.DMA((count,)),
+            pltpu.SemaphoreType.DMA((count,)),
+        ],
     )(where, *blocks)
 
 
@@ -138,7 +165,7 @@
             self.blocks, ring_member(self.mine + offset, self.size), 0, keepdims=False
         )
 
-    def step(self, *tokens):
+    def step(self, line):
         half = self.rows // 2
         if self.up is None:
             up = self.block(self.left)
@@ -150,8 +177,7 @@
                 down = jnp.concatenate([down[:half], add16(down[half:], self.down)])
             else:
                 up, down = add16(up, self.up), add16(down, self.down)
-        if tokens:
-            up, down = lax.optimization_barrier((up, down) + tokens)[:2]
+        up, down = line.pass_by(up, down)
         self.up = lax.ppermute(up, "dp", ring_pairs(self.size, 1))
         self.down = lax.ppermute(down, "dp", ring_pairs(self.size, -1))
         self.left -= 1
@@ -166,20 +192,37 @@
     return (left.astype(F32) + right.astype(F32)).astype(BF16)
 
 
-def gather_rows(rows):
-    across = swap(rows, "tensor", 4, 2)
-    beside = swap(rows, "tensor", 4, 1)
-    corner = swap(across, "tensor", 4, 1)
-    return jnp.concatenate([rows, beside, across, corner], 0)
-
-
-def scatter_rows(far, near):
-    rows = far.shape[0] // 2
-    far_in = swap(far[rows:], "tensor", 4, 1)
-    far_sum = add16(far[:rows], far_in)
-    across = swap(far_sum, "tensor", 4, 2)
-    near_in = swap(near[rows:], "tensor", 4, 1)
-    return near[:rows].astype(F32) + near_in.astype(F32) + across.astype(F32)
+class Rows:
+    def __init__(self, rows, line):
+        self.rows = line.pass_by(rows)
+        self.across = swap(self.rows, "tensor", 4, 2)
+        self.beside = swap(self.rows, "tensor", 4, 1)
+
+    def turn(self, line):
+        self.across = line.pass_by(self.across)
+        self.corner = swap(self.across, "tensor", 4, 1)
+
+    def whole(self):
+        return jnp.concatenate([self.rows, self.beside, self.across, self.corner], 0)
+
+
+class Sum:
+    def far(self, far, line):
+        rows = far.shape[0] // 2
+        self.far_own, far = far[:rows], line.pass_by(far[rows:])
+        self.far_in = swap(far, "tensor", 4, 1)
+
+    def turn(self, line):
+        self.across = swap(line.pass_by(add16(self.far_own, self.far_in)), "tensor", 4, 2)
+
+    def near(self, near, line):
+        rows = near.shape[0] // 2
+        self.near_own, near = near[:rows], line.pass_by(near[rows:])
+        self.near_in = swap(near, "tensor", 4, 1)
+
+    def result(self):
+        total = self.near_own.astype(F32) + self.near_in.astype(F32)
+        return total + self.across.astype(F32)
 
 
 def gather_small(vector, size):
@@ -206,33 +249,28 @@
 
 
 def attend(queries, keys, values, allowed, scale):
-    outs, saved = [], []
-    for low, high in ((0, 512), (512, 1024)):
-        scores = mm("qhd,kd->hqk", queries[low:high], keys) * scale
-        scores = jnp.where(allowed[None, low:high], scores, NEG_FILL)
-        row_max = jnp.max(scores, -1, keepdims=True)
-        shifted = jnp.exp(scores - row_max)
-        row_sum = jnp.sum(shifted, -1, keepdims=True)
-        low_probs = (shifted / row_sum).astype(BF16)
-        outs.append(mm("hqk,kd->qhd", low_probs, values).astype(BF16))
-        saved.append((row_max, row_sum))
-    return jnp.concatenate(outs, 0), saved
-
-
-def attend_back(queries, keys, values, grads, allowed, scale, saved):
-    grad_queries, grad_keys, grad_values = [], 0.0, 0.0
-    for (low, high), (row_max, row_sum) in zip(((0, 512), (512, 1024)), saved):
-        query, grad = queries[low:high], grads[low:high]
-        scores = mm("qhd,kd->hqk", query, keys) * scale
-        scores = jnp.where(allowed[None, low:high], scores, NEG_FILL)
-        probs = jnp.exp(scores - row_max) / row_sum
-        grad_probs = mm("qhd,kd->hqk", grad, values)
-        spread = jnp.sum(probs * grad_probs, -1, keepdims=True)
-        grad_scores = (probs * (grad_probs - spread)).astype(BF16)
-        grad_queries.append(mm("hqk,kd->qhd", grad_scores, keys) * scale)
-        grad_keys = grad_keys + mm("hqk,qhd->kd", grad_scores, query) * scale
-        grad_values = grad_values + mm("hqk,qhd->kd", probs.astype(BF16), grad)
-    return jnp.concatenate(grad_queries, 0), grad_keys, grad_values
+    scores = mm("qhd,kd->hqk", queries, keys) * scale
+    scores = jnp.where(allowed[None], scores, NEG_FILL)
+    row_max = jnp.max(scores, -1, keepdims=True)
+    shifted = jnp.exp(scores - row_max)
+    row_sum = jnp.sum(shifted, -1, keepdims=True)
+    low_probs = (shifted / row_sum).astype(BF16)
+    out = mm("hqk,kd->qhd", low_probs, values).astype(BF16)
+    return out.reshape(queries.shape[0], -1), (row_max, row_sum)
+
+
+def attend_back(query, keys, values, grad, allowed, scale, saved):
+    row_max, row_sum = saved
+    scores = mm("qhd,kd->hqk", query, keys) * scale
+    scores = jnp.where(allowed[None], scores, NEG_FILL)
+    probs = jnp.exp(scores - row_max) / row_sum
+    grad_probs = mm("qhd,kd->hqk", grad, values)
+    spread = jnp.sum(probs * grad_probs, -1, keepdims=True)
+    grad_scores = (probs * (grad_probs - spread)).astype(BF16)
+    grad_query = mm("hqk,kd->qhd", grad_scores, keys) * scale
+    grad_keys = mm("hqk,qhd->kd", grad_scores, query) * scale
+    grad_values = mm("hqk,qhd->kd", probs.astype(BF16), grad)
+    return grad_query, grad_keys, grad_values
 
 
 def body(
@@ -316,36 +354,36 @@
     kv_rows = jnp.take(kv_rel, jnp.arange(groups, dtype=jnp.int32) ^ tensor_index, axis=0)
     kv_rows = kv_rows.reshape(shard_rows, 2 * HEAD_SIZE)
 
-    states_all = gather_rows(states)
-    ring_q = Gather(w_query, dp_size)
-    ring_kv = Gather(kv_rows, dp_size)
-    ring_o = Gather(w_output.T, dp_size)
+    steps = dp_size // 2
+    line = Line()
     ring_gate = Gather(w_gate, dp_size)
     ring_up = Gather(w_up, dp_size)
     ring_down = Gather(w_down.T, dp_size)
-    window = []
-
-    def go(ring, steps):
-        for _ in range(steps):
-            tokens = window[-2] if len(window) >= 2 else ()
-            window.append(ring.step(*tokens))
-
-    steps = dp_size // 2
-    for _ in range(steps):
-        ring_q.step()
-        ring_kv.step()
-        ring_o.step()
-    window.append(ring_q.ups[-2:-1])
-    for _ in range(steps):
-        go(ring_gate, 1)
-        go(ring_up, 1)
-    go(ring_down, steps)
-
-    states_f = states_all.astype(F32)
+    ring_att = Gather(jnp.concatenate([w_query, kv_rows, w_output.T], 1), dp_size)
+    rows_one = Rows(states, line)
+    for _ in range(steps - 1):
+        ring_att.step(line)
+    rows_one.turn(line)
+    ring_att.step(line)
+    queue = [ring_gate, ring_up] * (steps - 1) + [ring_down, ring_gate, ring_up]
+    queue += [ring_down] * (steps - 1)
+
+    def send(count):
+        for _ in range(count):
+            queue.pop(0).step(line)
+
+    send(2 * (steps - 3))
+
+    half = all_rows // 2
+    states_f = rows_one.whole().astype(F32)
     rms_one = lax.rsqrt(jnp.mean(states_f * states_f, -1, keepdims=True) + NORM_EPS)
     normed_all = (states_f * rms_one * gain_one).astype(BF16)
-    w_qkv = jnp.concatenate([ring_q.whole(), ring_kv.whole()], 1)
-    qkv = jnp.dot(normed_all, w_qkv, preferred_element_type=F32) + qkv_bias
+    w_att = ring_att.whole()
+    qkv_cols = head_cols + 2 * HEAD_SIZE
+    w_qkv, output_t = w_att[:, :qkv_cols], w_att[:, qkv_cols:]
+    qkv = jnp.dot(line.hold(normed_all), w_qkv, preferred_element_type=F32) + qkv_bias
+    line.mark(qkv)
+    send(1)
     cosine, sine = tables(positions)
     queries = rotate(
         qkv[:, :head_cols].reshape(all_rows, local_heads, HEAD_SIZE),
@@ -356,111 +394,184 @@
     values = qkv[:, head_cols + HEAD_SIZE :].astype(BF16)
     allowed = (positions[None, :] <= positions[:, None]) | (positions[None, :] < prefix_len[0])
     allowed = allowed & (valid_all[None, :] > 0)
-    attended, saved = attend(queries, keys, values, allowed, score_scale)
-    attended = attended.reshape(all_rows, head_cols)
-    output_t = ring_o.whole()
-    half = all_rows // 2
-    far = mm("rh,dh->rd", attended[half:], output_t).astype(BF16)
-    near = mm("rh,dh->rd", attended[:half], output_t).astype(BF16)
+    sum_one = Sum()
+    attended_far, saved_far = attend(
+        line.hold(queries[half:]), keys, values, allowed[half:], score_scale
+    )
+    far = mm("rh,dh->rd", attended_far, output_t).astype(BF16)
+    line.mark(far)
+    sum_one.far(far, line)
+    send(1)
+    attended_near, saved_near = attend(
+        line.hold(queries[:half]), keys, values, allowed[:half], score_scale
+    )
+    line.mark(attended_near)
+    sum_one.turn(line)
+    near = mm("rh,dh->rd", line.hold(attended_near), output_t).astype(BF16)
+    sum_one.near(near, line)
+    send(1)
     states_own = states_f[:row_count]
-    middle = states_own + scatter_rows(far, near)
+    middle = states_own + sum_one.result()
 
     rms_two = lax.rsqrt(jnp.mean(middle * middle, -1, keepdims=True) + NORM_EPS)
     normed_two = (middle * rms_two * gain_two).astype(BF16)
-    normed_two_all = gather_rows(normed_two)
+    rows_two = Rows(normed_two, line)
+    send(2)
+    rows_two.turn(line)
+    send(2)
+    normed_two_all = rows_two.whole()
     gate_w, up_w = ring_gate.whole(), ring_up.whole()
-    gate_act = jnp.dot(normed_two_all, gate_w, preferred_element_type=F32)
-    up_act = jnp.dot(normed_two_all, up_w, preferred_element_type=F32)
+    gate_act = jnp.dot(line.hold(normed_two_all), gate_w, preferred_element_type=F32)
+    line.mark(gate_act)
+    send(1)
+    up_act = jnp.dot(line.hold(normed_two_all), up_w, preferred_element_type=F32)
     sigma = jax.nn.sigmoid(gate_act)
     hidden = (gate_act * sigma * up_act).astype(BF16)
+    line.mark(hidden)
+    send(len(queue))
     down_t = ring_down.whole()
+    sum_two = Sum()
     far = mm("rf,df->rd", hidden[half:], down_t).astype(BF16)
-    near = mm("rf,df->rd", hidden[:half], down_t).astype(BF16)
-    result = middle + scatter_rows(far, near)
+    line.mark(far)
+    sum_two.far(far, line)
+    near = mm("rf,df->rd", line.hold(hidden[:half]), down_t).astype(BF16)
+    line.mark(near)
+    sum_two.turn(line)
+    sum_two.near(near, line)
+    result = middle + sum_two.result()
 
     deviation = result - teacher.astype(F32)
     square_sum = jnp.sum(valid_rows * deviation * deviation)
     token_total = float(all_rows * dp_size)
     grad_result = cotangent.astype(F32) + token_total / count_all * valid_rows * deviation
 
-    grad_two_all = gather_rows(grad_result.astype(BF16))
+    rows_back = Rows(grad_result.astype(BF16), line)
+
+    def weight_grad(left, right):
+        product = mm("rd,rf->df", left, right).astype(BF16)
+        return with_layout_constraint(product, Layout(major_to_minor=(0, 1)))
 
     def split(gradient):
-        return gradient.astype(BF16).reshape(dp_size, shard_rows, -1)
-
-    grad_down = mm("rd,rf->df", grad_two_all, hidden)
+        return gradient.reshape(dp_size, shard_rows, -1)
+
+    def gate_back(grads, part):
+        grad_hidden = mm("rd,df->rf", grads, down_t)
+        gate, up, sig = gate_act[part], up_act[part], sigma[part]
+        grad_gate = grad_hidden * up * sig * (1.0 + gate * (1.0 - sig))
+        grad_up = grad_hidden * gate * sig
+        return grad_gate.astype(BF16), grad_up.astype(BF16)
+
+    def normed_back(gate_grads, up_grads):
+        total = mm("rf,df->rd", gate_grads, gate_w) + mm("rf,df->rd", up_grads, up_w)
+        return total.astype(BF16)
+
+    near_part, far_part = slice(0, half), slice(half, all_rows)
+    near_grads = jnp.concatenate([rows_back.rows, line.hold(rows_back.beside)], 0)
+    gate_near, up_near = gate_back(near_grads, near_part)
+    line.mark(gate_near, up_near)
+    rows_back.turn(line)
+    grad_two_all = rows_back.whole()
+    grad_down = weight_grad(line.hold(grad_two_all), hidden)
+    line.mark(grad_down)
     sum_down = Scatter(split(grad_down), dp_size)
-    grad_hidden = mm("rd,df->rf", grad_two_all, down_t)
-    grad_gate_act = (grad_hidden * up_act * sigma * (1.0 + gate_act * (1.0 - sigma))).astype(BF16)
-    grad_up_act = (grad_hidden * gate_act * sigma).astype(BF16)
-    sum_gate = Scatter(split(mm("rd,rf->df", normed_two_all, grad_gate_act)), dp_size)
-    sum_up = Scatter(split(mm("rd,rf->df", normed_two_all, grad_up_act)), dp_size)
-    far = mm("rf,df->rd", grad_gate_act[half:], gate_w)
-    far = (far + mm("rf,df->rd", grad_up_act[half:], up_w)).astype(BF16)
-    near = mm("rf,df->rd", grad_gate_act[:half], gate_w)
-    near = (near + mm("rf,df->rd", grad_up_act[:half], up_w)).astype(BF16)
-    grad_normed_two = scatter_rows(far, near)
+    sum_down.step(line)
+    gate_far, up_far = gate_back(line.hold(grad_two_all[half:]), far_part)
+    line.mark(gate_far, up_far)
+    sum_down.step(line)
+    sum_back = Sum()
+    far = normed_back(line.hold(gate_far), up_far)
+    line.mark(far)
+    sum_back.far(far, line)
+    grad_gate = weight_grad(
+        line.hold(normed_two_all), jnp.concatenate([gate_near, gate_far], 0)
+    )
+    line.mark(grad_gate)
+    sum_gate = Scatter(split(grad_gate), dp_size)
+    sum_back.turn(line)
+    for _ in range(steps - 3):
+        sum_down.step(line)
+    sum_gate.step(line)
+    near = normed_back(line.hold(gate_near), up_near)
+    line.mark(near)
+    sum_back.near(near, line)
+    grad_up = weight_grad(line.hold(normed_two_all), jnp.concatenate([up_near, up_far], 0))
+    line.mark(grad_up)
+    sum_up = Scatter(split(grad_up), dp_size)
+    sum_up.step(line)
+    sum_down.step(line)
+    grad_normed_two = sum_back.result()
     scaled_two = middle * rms_two
     grad_gain_two = jnp.sum(grad_normed_two * scaled_two, 0)
     pulled = gain_two * grad_normed_two
     grad_middle = grad_result + rms_two * (
         pulled - scaled_two * jnp.mean(pulled * scaled_two, -1, keepdims=True)
     )
-    grad_one_all = gather_rows(grad_middle.astype(BF16))
-    sum_o = Scatter(split(mm("rd,rh->dh", grad_one_all, attended)), dp_size)
+    rows_mid = Rows(grad_middle.astype(BF16), line)
+    for _ in range(steps - 3):
+        sum_gate.step(line)
+    rows_mid.turn(line)
+    for _ in range(steps - 3):
+        sum_up.step(line)
+    grad_one_all = line.hold(rows_mid.whole())
     grad_attended = mm("rd,dh->rh", grad_one_all, output_t).astype(BF16)
-    grad_queries, grad_keys, grad_values = attend_back(
-        queries,
-        keys,
-        values,
-        grad_attended.reshape(all_rows, local_heads, HEAD_SIZE),
-        allowed,
-        score_scale,
-        saved,
-    )
+    grad_attended = grad_attended.reshape(all_rows, local_heads, HEAD_SIZE)
+
+    def back(part, saved):
+        return attend_back(
+            line.hold(queries[part]),
+            keys,
+            values,
+            grad_attended[part],
+            allowed[part],
+            score_scale,
+            saved,
+        )
+
+    back_far = back(far_part, saved_far)
+    line.mark(*back_far)
+    sum_gate.step(line)
+    back_near = back(near_part, saved_near)
+    line.mark(*back_near)
+    grad_queries = jnp.concatenate([back_near[0], back_far[0]], 0)
+    grad_keys, grad_values = back_near[1] + back_far[1], back_near[2] + back_far[2]
     grad_query_raw = rotate(grad_queries, cosine[:, None, :], -sine[:, None, :]).astype(BF16)
     grad_key_raw = rotate(grad_keys, cosine, -sine).astype(BF16)
     grad_qkv = jnp.concatenate(
         [grad_query_raw.reshape(all_rows, head_cols), grad_key_raw, grad_values.astype(BF16)], 1
     )
-    sum_qkv = Scatter(split(mm("rd,rf->df", normed_all, grad_qkv)), dp_size)
+    attended = jnp.concatenate([attended_near, attended_far], 0)
+    grad_o = weight_grad(grad_one_all, attended)
+    grad_w_qkv = weight_grad(normed_all, grad_qkv)
+    grad_att = line.hold(jnp.concatenate([grad_w_qkv, grad_o], 1))
+    line.mark(grad_att)
+    sum_att = Scatter(split(grad_att), dp_size)
+    sum_att.step(line)
     grad_qkv_bias = jnp.sum(grad_qkv.astype(F32), 0)
-    grad_normed_part = mm("rf,df->rd", grad_qkv, w_qkv)
+    grad_normed_part = mm("rf,df->rd", line.hold(grad_qkv), w_qkv)
     scaled_one = states_f * rms_one
     grad_gain_one = jnp.sum(grad_normed_part * scaled_one, 0)
     grad_normed_part = grad_normed_part.astype(BF16)
-    grad_normed = scatter_rows(grad_normed_part[half:], grad_normed_part[:half])
+    line.mark(grad_normed_part)
+    sum_last = Sum()
+    sum_last.far(grad_normed_part[half:], line)
+    sum_last.near(grad_normed_part[:half], line)
+    sum_last.turn(line)
+    sum_up.step(line)
+    for _ in range(steps - 3):
+        sum_att.step(line)
+    sum_gate.step(line)
+    grad_normed = sum_last.result()
     pulled = gain_one * grad_normed
     scaled_own = scaled_one[:row_count]
     grad_states = grad_middle + rms_one[:row_count] * (
         pulled - scaled_own * jnp.mean(pulled * scaled_own, -1, keepdims=True)
     )
-
-    window.clear()
-
-    def send(ring, steps):
-        for _ in range(steps):
-            tokens = window[-2] if len(window) >= 2 else ()
-            window.append(ring.step(*tokens))
-
-    send(sum_down, 1)
-    send(sum_down, 1)
-    for _ in range(steps - 2):
-        send(sum_down, 1)
-        send(sum_gate, 1)
-    send(sum_gate, 1)
-    send(sum_up, 1)
-    send(sum_gate, 1)
-    send(sum_up, 1)
-    for _ in range(steps - 2):
-        send(sum_up, 1)
-        send(sum_o, 1)
-    for _ in range(2):
-        sum_o.step()
-    for _ in range(steps):
-        sum_qkv.step()
-
-    qkv_sum = sum_qkv.result()
+    sum_att.step(line)
+    sum_up.step(line)
+    sum_att.step(line)
+
+    att_sum = sum_att.result()
+    qkv_sum, o_sum = att_sum[:, :qkv_cols], att_sum[:, qkv_cols:]
     grad_w_query = qkv_sum[:, :head_cols]
     kv_sum = qkv_sum[:, head_cols:].reshape(groups, shard_rows // groups, 2 * HEAD_SIZE)
     kv_rel = [lax.dynamic_index_in_dim(kv_sum, b, 0, keepdims=False) for b in blocks]
@@ -502,7 +613,7 @@
         grad_w_query,
         grad_w_key,
         grad_w_value,
-        sum_o.result().T,
+        o_sum.T,
         sum_gate.result(),
         sum_up.result(),
         sum_down.result().T,

time: 1510 us -> 734 us (0.49)
  Pallas kernels: 750 us -> 23 us
  local copies, waits for them, and re-layouts: 79.2 us -> 45 us
  starting transfers between devices: 116 us -> 92.6 us
  waiting for transfers between devices: 285 us -> 304 us
    pallas_call x6 -> x4, Pallas kernels: 750 us -> 23 us  [place(): pl.pallas_call(functools.partial(place_kernel, spans), out_shape=jax.Shap...]
    ppermute x38, waiting for transfers between devices: 54.9 us -> 129 us  [swap(): return lax.ppermute(value, axis, [(i, i ^ bits) for i in range(size)])]
    ppermute x20 -> x16, waiting for transfers between devices: 70.5 us -> 24.5 us  [step(): self.down = lax.ppermute(down, 'dp', ring_pairs(self.size, -1))]
    convert_element_type x3 -> x0, local copies, waits for them, and re-layouts: 29.3 us -> none  [split(): return gradient.astype(BF16).reshape(dp_size, shard_rows, -1)]
    ppermute x24 -> x16, waiting for transfers between devices: 80.7 us -> 61.9 us  [step(): self.up = lax.ppermute(up, 'dp', ring_pairs(size, 1))]
    ppermute x24 -> x16, starting transfers between devices: 32.3 us -> 25.2 us  [step(): self.up = lax.ppermute(up, 'dp', ring_pairs(size, 1))]
    ppermute x20 -> x16, waiting for transfers between devices: 63 us -> 69.7 us  [step(): self.up = lax.ppermute(up, 'dp', ring_pairs(self.size, 1))]
    dot_general x26 -> x31, matrix products: 134 us -> 135 us  [mm(): return jnp.einsum(spec, left, right, preferred_element_type=F32)]
  transfers between devices with their start and end apart: 126 -> 102, of which waited for: 52 -> 52; matrix products, arithmetic and copies ran while one was open for 18% -> 35% of each run, Pallas kernels for 36% -> 2%
where the time goes in v2:
time: 734 us; the launch traced here: 724 us
  waiting for transfers between devices  304 us (41%)
  matrix products  169 us (23%)
  starting transfers between devices  92.6 us (13%)
  other arithmetic  83.2 us (11%)
  local copies, waits for them, and re-layouts  45 us (6%)
  Pallas kernels  23 us (3%)
    dot_general x31, matrix products, mm(): return jnp.einsum(spec, left, right, preferred_element_type=F32)  135 us
    ppermute x38, waiting for transfers between devices, swap(): return lax.ppermute(value, axis, [(i, i ^ bits) for i in range(size)])  129 us
    ppermute x16, waiting for transfers between devices, step(): self.up = lax.ppermute(up, 'dp', ring_pairs(self.size, 1))  69.7 us
    ppermute x16, waiting for transfers between devices, step(): self.up = lax.ppermute(up, 'dp', ring_pairs(size, 1))  61.9 us
    convert_element_type x16, other arithmetic, add16(): return (left.astype(F32) + right.astype(F32)).astype(BF16)  27 us
    ppermute x16, starting transfers between devices, step(): self.down = lax.ppermute(down, 'dp', ring_pairs(self.size, -1))  25.4 us
    ppermute x16, starting transfers between devices, step(): self.up = lax.ppermute(up, 'dp', ring_pairs(size, 1))  25.2 us
    ppermute x38, starting transfers between devices, swap(): return lax.ppermute(value, axis, [(i, i ^ bits) for i in range(size)])  24.6 us
  transfers between devices with their start and end apart: 102, of which 52 were waited for; matrix products, arithmetic and copies ran while one was open for 35% of the time, Pallas kernels for 2%

profile of v2, /device:TPU:0, one launch (start us, length us, event | category | flops | bytes accessed | tf_op | source)
XLA Modules:
  0.0 724.2 jit_solution(2997419700673699739)
XLA Ops:
  8.7 3.4 concatenate.144
  14.5 7.4 %collective-permute-done.2 = bf16[48,256]{1,0:T(8,128)(2,1)S(1)} collective-permute-done((bf16[48,256]{1,0:T(8,128)(2,1)S(1)}, bf16[48,256]{1,0:T(8,128)(2,1)S(1)}, u32[]{:S(2)}, u32[]{:S(2)}) %collective-permute-start.2) | collective-permute-done | bytes 24608 | tf_op jit(solution)/shard_map/ppermute | solution.py:66
  41.5 8.0 %collective-permute-done.12 = f32[8,161]{1,0:T(8,128)S(1)} collective-permute-done((f32[8,161]{1,0:T(8,128)S(1)}, f32[8,161]{1,0:T(8,128)S(1)}, u32[]{:S(2)}, u32[]{:S(2)}) %collective-permute-start.12) | collective-permute-done | bytes 5184 | tf_op jit(solution)/shard_map/ppermute | solution.py:66
  57.9 5.2 collective-permute-done.14.refs_3_
  76.7 3.4 shard_map.280
  82.3 5.5 multiply_convert_fusion.1
  93.0 3.7 collective-permute-done.21.refs_5_
  105.2 6.6 collective-permute-done.18.refs_1_
  111.8 3.8 collective-permute-done.19.refs_5_
  130.0 15.2 %collective-permute-done.24 = bf16[256,1536]{1,0:T(8,128)(2,1)} collective-permute-done((bf16[256,1536]{1,0:T(8,128)(2,1)}, bf16[256,1536]{1,0:T(8,128)(2,1)}, u32[]{:S(2)}, u32[]{:S(2)}) %collective-permute-start.24) | collective-permute-done | bytes 786464 | tf_op jit(solution)/shard_map/ppermute | solution.py:66
  153.5 13.1 %collective-permute-done.28 = bf16[256,1536]{1,0:T(8,128)(2,1)} collective-permute-done((bf16[256,1536]{1,0:T(8,128)(2,1)S(1)}, bf16[256,1536]{1,0:T(8,128)(2,1)}, u32[]{:S(2)}, u32[]{:S(2)}) %collective-permute-start.28) | collective-permute-done | bytes 786464 | tf_op jit(solution)/shard_map/ppermute | solution.py:66
  166.5 5.0 collective-permute-done.34.refs_3_
  174.4 16.1 %collective-permute-done.32.refs_3_ = bf16[192,2240]{1,0:T(8,128)(2,1)S(1)} collective-permute-done((bf16[192,2240]{1,0:T(8,128)(2,1)S(1)}, bf16[192,2240]{1,0:T(8,128)(2,1)S(1)}, u32[]{:S(2)}, u32[]{:S(2)}) %collective-permute-start.32) | collective-permute-done | bytes 860192 | tf_op jit(solution)/shard_map/ppermute | solution.py:98
  196.1 3.8 collective-permute-done.36.refs_4_
  204.9 6.5 shard_map.281
  213.1 6.5 shard_map.282
  221.8 13.2 %fusion.150 = f32[1024,2240]{0,1:T(8,128)} fusion(bf16[1024,1536]{1,0:T(8,128)(2,1)} %constant_dynamic-update-slice_fusion.2, bf16[1536,2240]{1,0:T(8,128)(2,1)} %bitcast.366), kind=kOutput, calls=%fused_computation.348 | convolution fusion | flops 7046430720 | bytes 19202048 | tf_op jit(solution)/shard_map/dot_general | solution.py:424
  237.0 18.2 %add_divide_fusion = (f32[1024,2240]{0,1:T(8,128)}, bf16[1024,2240]{0,1:T(8,128)(2,1)}, f32[1024,2240]{0,1:T(8,128)}) fusion(f32[1024,2240]{0,1:T(8,128)} %fusion.150, bf16[1024,1536]{1,0:T(8,128)(2,1)} %constant_dynamic-update-slice_fusion.2, bf16[1536,2240]{1,0:T(8,128)(2,1)} %bitcast.371), kind=kOutput, calls=%fused_computation.6 | convolution fusion | flops 7060193280 | bytes 42139648 | tf_op jit(solution)/shard_map/dot_general | solution.py:427
  258.2 17.0 %collective-permute-done.44.refs_3_ = bf16[192,2240]{1,0:T(8,128)(2,1)S(1)} collective-permute-done((bf16[192,2240]{1,0:T(8,128)(2,1)}, bf16[192,2240]{1,0:T(8,128)(2,1)S(1)}, u32[]{:S(2)}, u32[]{:S(2)}) %collective-permute-start.44) | collective-permute-done | bytes 860192 | tf_op jit(solution)/shard_map/ppermute | solution.py:98
  286.6 6.6 shard_map.283
  293.2 7.7 %convolution_convert_fusion.5 = bf16[512,1536]{1,0:T(8,128)(2,1)S(1)} fusion(bf16[1536,2240]{1,0:T(8,128)(2,1)} %bitcast.374, bf16[1024,2240]{0,1:T(8,128)(2,1)} %get-tuple-element.236), kind=kOutput, calls=%fused_computation.70 | convolution fusion | flops 3524001792 | bytes 10944512 | tf_op jit(solution)/shard_map/rf,df->rd/dot_general | solution.py:24
  301.1 3.9 convolution_convert_fusion.4
  308.6 17.5 %collective-permute-done.50 = bf16[256,1536]{1,0:T(8,128)(2,1)} collective-permute-done((bf16[256,1536]{1,0:T(8,128)(2,1)S(1)}, bf16[256,1536]{1,0:T(8,128)(2,1)}, u32[]{:S(2)}, u32[]{:S(2)}) %collective-permute-start.50) | collective-permute-done | bytes 786464 | tf_op jit(solution)/shard_map/ppermute | solution.py:66
  333.1 14.6 %multiply_convert_fusion.3 = (bf16[512,2240]{0,1:T(8,128)(2,1)}, bf16[512,2240]{0,1:T(8,128)(2,1)}) fusion(f32[1024,2240]{0,1:T(8,128)} %fusion.150, f32[1024,2240]{0,1:T(8,128)} %get-tuple-element.235, f32[1024,2240]{0,1:T(8,128)} %get-tuple-element.336, bf16[1536,2240]{1,0:T(8,128)(2,1)} %bitcast.375, bf16[256,1536]{1,0:T(8,128)(2,1)} %collective-permute-done.52, ...), kind=kOutput, calls=%fused_computation.53 | convolution fusion | flops 3537829888 | bytes 26804224 | tf_op jit(solution)/shard_map/rd,df->rf/dot_general | solution.py:24
  350.6 9.3 %fusion.152 = f32[512,1536]{1,0:T(8,128)} fusion(bf16[512,2240]{0,1:T(8,128)(2,1)} %get-tuple-element.233, bf16[1536,2240]{1,0:T(8,128)(2,1)} %bitcast.372), kind=kOutput, calls=%fused_computation.350 | convolution fusion | flops 3523215360 | bytes 12320768 | tf_op jit(solution)/shard_map/rf,df->rd/dot_general | solution.py:24
  361.4 10.3 %convolution_convert_fusion.2 = bf16[1536,2240]{1,0:T(8,128)(2,1)S(1)} fusion(bf16[1024,1536]{1,0:T(8,128)(2,1)S(1)} %pad_maximum_fusion, bf16[1024,2240]{0,1:T(8,128)(2,1)} %get-tuple-element.236), kind=kOutput, calls=%fused_computation.4 | convolution fusion | flops 7049871360 | bytes 14614528 | tf_op jit(solution)/shard_map/rd,rf->df/dot_general | solution.py:24
  377.7 13.4 %fusion.18 = (bf16[512,2240]{0,1:T(8,128)(2,1)}, bf16[512,2240]{0,1:T(8,128)(2,1)}) fusion(f32[1024,2240]{0,1:T(8,128)} %get-tuple-element.336, f32[1024,2240]{0,1:T(8,128)} %fusion.150, f32[1024,2240]{0,1:T(8,128)} %get-tuple-element.235, bf16[512,1536]{1,0:T(8,128)(2,1)S(1)} %pad_maximum_fusion.3, bf16[1536,2240]{1,0:T(8,128)(2,1)} %bitcast.376), kind=kOutput, calls=%fused_computation.41 | convolution fusion | flops 3534684160 | bytes 26804224 | tf_op jit(solution)/shard_map/rd,df->rf/dot_general | solution.py:24
  391.1 7.0 fusion.151
  403.4 3.9 fusion.34
  407.5 10.6 %convolution_convert_fusion.1 = bf16[1536,2240]{1,0:T(8,128)(2,1)S(1)} fusion(bf16[1024,1536]{1,0:T(8,128)(2,1)} %constant_dynamic-update-slice_fusion.2, bf16[512,2240]{0,1:T(8,128)(2,1)} %get-tuple-element.174, bf16[512,2240]{0,1:T(8,128)(2,1)} %get-tuple-element.182), kind=kOutput, calls=%fused_computation.3 | convolution fusion | flops 7059046400 | bytes 14614528 | tf_op jit(solution)/shard_map/rd,rf->df/dot_general | solution.py:24
  423.2 3.6 fusion.50
  431.0 6.3 fusion.35
  438.2 10.6 %convolution_convert_fusion = bf16[1536,2240]{1,0:T(8,128)(2,1)S(1)} fusion(bf16[1024,1536]{1,0:T(8,128)(2,1)} %constant_dynamic-update-slice_fusion.2, bf16[512,2240]{0,1:T(8,128)(2,1)} %get-tuple-element.232, bf16[512,2240]{0,1:T(8,128)(2,1)} %get-tuple-element.233), kind=kOutput, calls=%fused_computation.2 | convolution fusion | flops 7059046400 | bytes 14614528 | tf_op jit(solution)/shard_map/rd,rf->df/dot_general | solution.py:24
  449.0 8.7 %collective-permute-done.59 = bf16[96,2240]{1,0:T(8,128)(2,1)} collective-permute-done((bf16[96,2240]{1,0:T(8,128)(2,1)}, bf16[96,2240]{1,0:T(8,128)(2,1)}, u32[]{:S(2)}, u32[]{:S(2)}) %collective-permute-start.59) | collective-permute-done | bytes 430112 | tf_op jit(solution)/shard_map/ppermute | solution.py:181
  464.7 3.6 fusion.48
  476.5 11.0 %collective-permute-done.69 = bf16[256,1536]{1,0:T(8,128)(2,1)S(1)} collective-permute-done((bf16[256,1536]{1,0:T(8,128)(2,1)S(1)}, bf16[256,1536]{1,0:T(8,128)(2,1)S(1)}, u32[]{:S(2)}, u32[]{:S(2)}) %collective-permute-start.69) | collective-permute-done | bytes 786464 | tf_op jit(solution)/shard_map/ppermute | solution.py:66
  487.5 4.8 collective-permute-done.65
  495.0 3.6 convolution_convert_fusion.9
  529.1 5.5 fusion.132
  548.2 13.4 %collective-permute-done.74 = f32[41,128]{1,0:T(8,128)S(1)} collective-permute-done((f32[41,128]{1,0:T(8,128)S(1)}, f32[41,128]{1,0:T(8,128)S(1)}, u32[]{:S(2)}, u32[]{:S(2)}) %collective-permute-start.74) | collective-permute-done | bytes 21024 | tf_op jit(solution)/shard_map/ppermute | solution.py:66
  562.9 14.6 %collective-permute-done.75 = f32[41,128]{1,0:T(8,128)S(1)} collective-permute-done((f32[41,128]{1,0:T(8,128)S(1)}, f32[41,128]{1,0:T(8,128)S(1)}, u32[]{:S(2)}, u32[]{:S(2)}) %collective-permute-start.75) | collective-permute-done | bytes 21024 | tf_op jit(solution)/shard_map/ppermute | solution.py:66
  577.5 3.6 collective-permute-start.87
  585.8 15.3 %collective-permute-done.76 = f32[41,128]{1,0:T(8,128)S(1)} collective-permute-done((f32[41,128]{1,0:T(8,128)S(1)}, f32[41,128]{1,0:T(8,128)S(1)}, u32[]{:S(2)}, u32[]{:S(2)}) %collective-permute-start.76) | collective-permute-done | bytes 21024 | tf_op jit(solution)/shard_map/ppermute | solution.py:66
  616.7 24.3 %collective-permute-done.84 = bf16[192,1024]{1,0:T(8,128)(2,1)S(1)} collective-permute-done((bf16[192,1024]{1,0:T(8,128)(2,1)S(1)}, bf16[192,1024]{1,0:T(8,128)(2,1)S(1)}, u32[]{:S(2)}, u32[]{:S(2)}) %collective-permute-start.84) | collective-permute-done | bytes 393248 | tf_op jit(solution)/shard_map/ppermute | solution.py:181
  647.3 25.2 %collective-permute-done.88 = bf16[192,1024]{1,0:T(8,128)(2,1)S(1)} collective-permute-done((bf16[192,1024]{1,0:T(8,128)(2,1)S(1)}, bf16[192,1024]{1,0:T(8,128)(2,1)S(1)}, u32[]{:S(2)}, u32[]{:S(2)}) %collective-permute-start.88) | collective-permute-done | bytes 393248 | tf_op jit(solution)/shard_map/ppermute | solution.py:181
  682.1 6.5 collective-permute-done.92
  690.1 13.3 %collective-permute-done.93 = bf16[192,1024]{1,0:T(8,128)(2,1)S(1)} collective-permute-done((bf16[192,1024]{1,0:T(8,128)(2,1)S(1)}, bf16[192,1024]{1,0:T(8,128)(2,1)S(1)}, u32[]{:S(2)}, u32[]{:S(2)}) %collective-permute-start.93) | collective-permute-done | bytes 393248 | tf_op jit(solution)/shard_map/ppermute | solution.py:182
  712.0 8.2 %collective-permute-done.99 = bf16[192,2240]{1,0:T(8,128)(2,1)S(1)} collective-permute-done((bf16[192,2240]{1,0:T(8,128)(2,1)S(1)}, bf16[192,2240]{1,0:T(8,128)(2,1)S(1)}, u32[]{:S(2)}, u32[]{:S(2)}) %collective-permute-start.99) | collective-permute-done | bytes 860192 | tf_op jit(solution)/shard_map/ppermute | solution.py:182
  (575 shorter events, 268.3 us)
Async XLA Ops:
  0.6 56.4 %collective-permute-start.1 = (bf16[256,1536]{1,0:T(8,128)(2,1)}, bf16[256,1536]{1,0:T(8,128)(2,1)S(1)}, u32[]{:S(2)}, u32[]{:S(2)}) collective-permute-start(bf16[256,1536]{1,0:T(8,128)(2,1)} %param.17), channel_id=1, source_target_pairs={{0,2},{1,3},{2,0},{3,1},{4,6},{5,7},{6,4},{7,5},{8,10},{9,11},{10,... | collective-permute-start | bytes 2359304 | tf_op jit(solution)/shard_map/ppermute | solution.py:66
  3.7 76.4 %collective-permute-start = (bf16[256,1536]{1,0:T(8,128)(2,1)}, bf16[256,1536]{1,0:T(8,128)(2,1)S(1)}, u32[]{:S(2)}, u32[]{:S(2)}) collective-permute-start(bf16[256,1536]{1,0:T(8,128)(2,1)} %param.17), channel_id=1, source_target_pairs={{0,1},{1,0},{2,3},{3,2},{4,5},{5,4},{6,7},{7,6},{8,9},{9,8},{10,11... | collective-permute-start | bytes 2359304 | tf_op jit(solution)/shard_map/ppermute | solution.py:66
  57.0 24.5 %collective-permute-start.8 = (bf16[256,1536]{1,0:T(8,128)(2,1)S(1)}, bf16[256,1536]{1,0:T(8,128)(2,1)S(1)}, u32[]{:S(2)}, u32[]{:S(2)}) collective-permute-start(bf16[256,1536]{1,0:T(8,128)(2,1)S(1)} %collective-permute-done.1), channel_id=1, source_target_pairs={{0,1},{1,0},{2,3},{3,2},{4,5},{5,4},{6,7},{7,6},{8,9},{9,8},{10,11... | collective-permute-start | bytes 2359304 | tf_op jit(solution)/shard_map/ppermute | solution.py:66
  69.1 23.9 %collective-permute-start.20 = (bf16[192,2240]{1,0:T(8,128)(2,1)}, bf16[192,2240]{1,0:T(8,128)(2,1)}, u32[]{:S(2)}, u32[]{:S(2)}) collective-permute-start(bf16[192,2240]{1,0:T(8,128)(2,1)} %refs_0_.2), channel_id=1, source_target_pairs={{0,8},{8,16},{16,24},{24,28},{28,20},{20,12},{12,4},{4,0},{1,9},{9... | collective-permute-start | bytes 2580488 | tf_op jit(solution)/shard_map/ppermute | solution.py:98
  73.9 22.8 %collective-permute-start.21 = (bf16[192,2240]{1,0:T(8,128)(2,1)}, bf16[192,2240]{1,0:T(8,128)(2,1)}, u32[]{:S(2)}, u32[]{:S(2)}) collective-permute-start(bf16[192,2240]{1,0:T(8,128)(2,1)} %refs_0_.2), channel_id=1, source_target_pairs={{0,4},{8,0},{16,8},{24,16},{28,24},{20,28},{12,20},{4,12},{1,5},{9... | collective-permute-start | bytes 2580488 | tf_op jit(solution)/shard_map/ppermute | solution.py:99
  75.9 35.9 %collective-permute-start.18 = (bf16[192,2240]{1,0:T(8,128)(2,1)}, bf16[192,2240]{1,0:T(8,128)(2,1)}, u32[]{:S(2)}, u32[]{:S(2)}) collective-permute-start(bf16[192,2240]{1,0:T(8,128)(2,1)} %refs_0_.3), channel_id=1, source_target_pairs={{0,8},{8,16},{16,24},{24,28},{28,20},{20,12},{12,4},{4,0},{1,9},{9... | collective-permute-start | bytes 2580488 | tf_op jit(solution)/shard_map/ppermute | solution.py:98
  80.1 35.5 %collective-permute-start.19 = (bf16[192,2240]{1,0:T(8,128)(2,1)}, bf16[192,2240]{1,0:T(8,128)(2,1)S(1)}, u32[]{:S(2)}, u32[]{:S(2)}) collective-permute-start(bf16[192,2240]{1,0:T(8,128)(2,1)} %refs_0_.3), channel_id=1, source_target_pairs={{0,4},{8,0},{16,8},{24,16},{28,24},{20,28},{12,20},{4,12},{1,5},{9... | collective-permute-start | bytes 2580488 | tf_op jit(solution)/shard_map/ppermute | solution.py:99
  96.8 33.2 %collective-permute-start.25 = (bf16[192,2240]{1,0:T(8,128)(2,1)}, bf16[192,2240]{1,0:T(8,128)(2,1)}, u32[]{:S(2)}, u32[]{:S(2)}) collective-permute-start(bf16[192,2240]{1,0:T(8,128)(2,1)} %collective-permute-done.20.refs_1_), channel_id=1, source_target_pairs={{0,8},{8,16},{16,24},{24,28},{28,20},{20,12},{12,4},{4,0},{1,9},{9... | collective-permute-start | bytes 2580488 | tf_op jit(solution)/shard_map/ppermute | solution.py:98
  98.8 31.2 %collective-permute-start.26 = (bf16[192,2240]{1,0:T(8,128)(2,1)}, bf16[192,2240]{1,0:T(8,128)(2,1)}, u32[]{:S(2)}, u32[]{:S(2)}) collective-permute-start(bf16[192,2240]{1,0:T(8,128)(2,1)} %collective-permute-done.21.refs_5_), channel_id=1, source_target_pairs={{0,4},{8,0},{16,8},{24,16},{28,24},{20,28},{12,20},{4,12},{1,5},{9... | collective-permute-start | bytes 2580488 | tf_op jit(solution)/shard_map/ppermute | solution.py:99
  127.8 23.0 %collective-permute-start.29 = (bf16[192,2240]{1,0:T(8,128)(2,1)}, bf16[192,2240]{1,0:T(8,128)(2,1)S(1)}, u32[]{:S(2)}, u32[]{:S(2)}) collective-permute-start(bf16[192,2240]{1,0:T(8,128)(2,1)} %collective-permute-done.18.refs_1_), channel_id=1, source_target_pairs={{0,8},{8,16},{16,24},{24,28},{28,20},{20,12},{12,4},{4,0},{1,9},{9... | collective-permute-start | bytes 2580488 | tf_op jit(solution)/shard_map/ppermute | solution.py:98
  148.8 22.7 %collective-permute-start.34 = (bf16[192,2240]{1,0:T(8,128)(2,1)}, bf16[192,2240]{1,0:T(8,128)(2,1)S(1)}, u32[]{:S(2)}, u32[]{:S(2)}) collective-permute-start(bf16[192,2240]{1,0:T(8,128)(2,1)} %collective-permute-done.25.refs_2_), channel_id=1, source_target_pairs={{0,8},{8,16},{16,24},{24,28},{28,20},{20,12},{12,4},{4,0},{1,9},{9... | collective-permute-start | bytes 2580488 | tf_op jit(solution)/shard_map/ppermute | solution.py:98
  150.8 22.7 %collective-permute-start.35 = (bf16[192,2240]{1,0:T(8,128)(2,1)}, bf16[192,2240]{1,0:T(8,128)(2,1)S(1)}, u32[]{:S(2)}, u32[]{:S(2)}) collective-permute-start(bf16[192,2240]{1,0:T(8,128)(2,1)} %collective-permute-done.26.refs_6_), channel_id=1, source_target_pairs={{0,4},{8,0},{16,8},{24,16},{28,24},{20,28},{12,20},{4,12},{1,5},{9... | collective-permute-start | bytes 2580488 | tf_op jit(solution)/shard_map/ppermute | solution.py:99
  151.4 39.1 %collective-permute-start.32 = (bf16[192,2240]{1,0:T(8,128)(2,1)S(1)}, bf16[192,2240]{1,0:T(8,128)(2,1)S(1)}, u32[]{:S(2)}, u32[]{:S(2)}) collective-permute-start(bf16[192,2240]{1,0:T(8,128)(2,1)S(1)} %collective-permute-done.29.refs_2_), channel_id=1, source_target_pairs={{0,8},{8,16},{16,24},{24,28},{28,20},{20,12},{12,4},{4,0},{1,9},{9... | collective-permute-start | bytes 2580488 | tf_op jit(solution)/shard_map/ppermute | solution.py:98
  152.9 39.0 %collective-permute-start.33 = (bf16[192,2240]{1,0:T(8,128)(2,1)S(1)}, bf16[192,2240]{1,0:T(8,128)(2,1)S(1)}, u32[]{:S(2)}, u32[]{:S(2)}) collective-permute-start(bf16[192,2240]{1,0:T(8,128)(2,1)S(1)} %collective-permute-done.30.refs_6_), channel_id=1, source_target_pairs={{0,4},{8,0},{16,8},{24,16},{28,24},{20,28},{12,20},{4,12},{1,5},{9... | collective-permute-start | bytes 2580488 | tf_op jit(solution)/shard_map/ppermute | solution.py:99
  166.5 27.8 %collective-permute-start.27 = (bf16[256,1536]{1,0:T(8,128)(2,1)S(1)}, bf16[256,1536]{1,0:T(8,128)(2,1)S(1)}, u32[]{:S(2)}, u32[]{:S(2)}) collective-permute-start(bf16[256,1536]{1,0:T(8,128)(2,1)S(1)} %multiply_convert_fusion.4), channel_id=1, source_target_pairs={{0,1},{1,0},{2,3},{3,2},{4,5},{5,4},{6,7},{7,6},{8,9},{9,8},{10,11... | collective-permute-start | bytes 2359304 | tf_op jit(solution)/shard_map/ppermute | solution.py:66
  171.5 48.1 %collective-permute-start.31 = (bf16[256,1536]{1,0:T(8,128)(2,1)}, bf16[256,1536]{1,0:T(8,128)(2,1)}, u32[]{:S(2)}, u32[]{:S(2)}) collective-permute-start(bf16[256,1536]{1,0:T(8,128)(2,1)} %collective-permute-done.28), channel_id=1, source_target_pairs={{0,1},{1,0},{2,3},{3,2},{4,5},{5,4},{6,7},{7,6},{8,9},{9,8},{10,11... | collective-permute-start | bytes 2359304 | tf_op jit(solution)/shard_map/ppermute | solution.py:66
  173.6 26.4 %collective-permute-start.36 = (bf16[96,2240]{1,0:T(8,128)(2,1)S(1)}, bf16[96,2240]{1,0:T(8,128)(2,1)S(1)}, u32[]{:S(2)}, u32[]{:S(2)}) collective-permute-start(bf16[96,2240]{1,0:T(8,128)(2,1)S(1)} %slice.524), channel_id=1, source_target_pairs={{0,8},{8,16},{16,24},{24,28},{28,20},{20,12},{12,4},{4,0},{1,9},{9... | collective-permute-start | bytes 1290248 | tf_op jit(solution)/shard_map/ppermute | solution.py:98
  200.0 34.9 %collective-permute-start.38 = (bf16[192,2240]{1,0:T(8,128)(2,1)}, bf16[192,2240]{1,0:T(8,128)(2,1)S(1)}, u32[]{:S(2)}, u32[]{:S(2)}) collective-permute-start(bf16[192,2240]{1,0:T(8,128)(2,1)} %bitcast.33.refs_0_), channel_id=1, source_target_pairs={{0,8},{8,16},{16,24},{24,28},{28,20},{20,12},{12,4},{4,0},{1,9},{9... | collective-permute-start | bytes 2580488 | tf_op jit(solution)/shard_map/ppermute | solution.py:98
  204.3 30.6 %collective-permute-start.39 = (bf16[192,2240]{1,0:T(8,128)(2,1)}, bf16[192,2240]{1,0:T(8,128)(2,1)}, u32[]{:S(2)}, u32[]{:S(2)}) collective-permute-start(bf16[192,2240]{1,0:T(8,128)(2,1)} %bitcast.33.refs_0_), channel_id=1, source_target_pairs={{0,4},{8,0},{16,8},{24,16},{28,24},{20,28},{12,20},{4,12},{1,5},{9... | collective-permute-start | bytes 2580488 | tf_op jit(solution)/shard_map/ppermute | solution.py:99
  375.6 22.6 %collective-permute-start.54 = (bf16[96,2240]{1,0:T(8,128)(2,1)}, bf16[96,2240]{1,0:T(8,128)(2,1)}, u32[]{:S(2)}, u32[]{:S(2)}) collective-permute-start(bf16[96,2240]{1,0:T(8,128)(2,1)} %get-tuple-element.169), channel_id=1, source_target_pairs={{0,8},{8,16},{16,24},{24,28},{28,20},{20,12},{12,4},{4,0},{1,9},{9... | collective-permute-start | bytes 1290248 | tf_op jit(solution)/shard_map/ppermute | solution.py:181
  422.0 37.9 %collective-permute-start.62 = (bf16[256,1536]{1,0:T(8,128)(2,1)}, bf16[256,1536]{1,0:T(8,128)(2,1)S(1)}, u32[]{:S(2)}, u32[]{:S(2)}) collective-permute-start(bf16[256,1536]{1,0:T(8,128)(2,1)} %add_convert_fusion.1), channel_id=1, source_target_pairs={{0,2},{1,3},{2,0},{3,1},{4,6},{5,7},{6,4},{7,5},{8,10},{9,11},{10,... | collective-permute-start | bytes 2359304 | tf_op jit(solution)/shard_map/ppermute | solution.py:66
  426.8 37.9 %collective-permute-start.63 = (bf16[192,2240]{1,0:T(8,128)(2,1)}, bf16[192,2240]{1,0:T(8,128)(2,1)}, u32[]{:S(2)}, u32[]{:S(2)}) collective-permute-start(bf16[192,2240]{1,0:T(8,128)(2,1)} %get-tuple-element.178), channel_id=1, source_target_pairs={{0,8},{8,16},{16,24},{24,28},{28,20},{20,12},{12,4},{4,0},{1,9},{9... | collective-permute-start | bytes 2580488 | tf_op jit(solution)/shard_map/ppermute | solution.py:181
  427.3 37.4 %collective-permute-start.64 = (bf16[192,2240]{1,0:T(8,128)(2,1)}, bf16[192,2240]{1,0:T(8,128)(2,1)}, u32[]{:S(2)}, u32[]{:S(2)}) collective-permute-start(bf16[192,2240]{1,0:T(8,128)(2,1)} %get-tuple-element.179), channel_id=1, source_target_pairs={{0,4},{8,0},{16,8},{24,16},{28,24},{20,28},{12,20},{4,12},{1,5},{9... | collective-permute-start | bytes 2580488 | tf_op jit(solution)/shard_map/ppermute | solution.py:182
  428.8 28.9 %collective-permute-start.59 = (bf16[96,2240]{1,0:T(8,128)(2,1)}, bf16[96,2240]{1,0:T(8,128)(2,1)}, u32[]{:S(2)}, u32[]{:S(2)}) collective-permute-start(bf16[96,2240]{1,0:T(8,128)(2,1)} %get-tuple-element.180), channel_id=1, source_target_pairs={{0,8},{8,16},{16,24},{24,28},{28,20},{20,12},{12,4},{4,0},{1,9},{9... | collective-permute-start | bytes 1290248 | tf_op jit(solution)/shard_map/ppermute | solution.py:181
  429.3 28.6 %collective-permute-start.60 = (bf16[96,2240]{1,0:T(8,128)(2,1)}, bf16[96,2240]{1,0:T(8,128)(2,1)}, u32[]{:S(2)}, u32[]{:S(2)}) collective-permute-start(bf16[96,2240]{1,0:T(8,128)(2,1)} %get-tuple-element.181), channel_id=1, source_target_pairs={{0,4},{8,0},{16,8},{24,16},{28,24},{20,28},{12,20},{4,12},{1,5},{9... | collective-permute-start | bytes 1290248 | tf_op jit(solution)/shard_map/ppermute | solution.py:182
  469.7 22.5 %collective-permute-start.65 = (bf16[192,2240]{1,0:T(8,128)(2,1)S(1)}, bf16[192,2240]{1,0:T(8,128)(2,1)S(1)}, u32[]{:S(2)}, u32[]{:S(2)}) collective-permute-start(bf16[192,2240]{1,0:T(8,128)(2,1)S(1)} %pad_maximum_fusion.7), channel_id=1, source_target_pairs={{0,8},{8,16},{16,24},{24,28},{28,20},{20,12},{12,4},{4,0},{1,9},{9... | collective-permute-start | bytes 2580488 | tf_op jit(solution)/shard_map/ppermute | solution.py:181
  470.2 22.5 %collective-permute-start.66 = (bf16[192,2240]{1,0:T(8,128)(2,1)S(1)}, bf16[192,2240]{1,0:T(8,128)(2,1)S(1)}, u32[]{:S(2)}, u32[]{:S(2)}) collective-permute-start(bf16[192,2240]{1,0:T(8,128)(2,1)S(1)} %pad_maximum_fusion.8), channel_id=1, source_target_pairs={{0,4},{8,0},{16,8},{24,16},{28,24},{20,28},{12,20},{4,12},{1,5},{9... | collective-permute-start | bytes 2580488 | tf_op jit(solution)/shard_map/ppermute | solution.py:182
  474.5 69.2 %collective-permute-start.100 = (bf16[192,2240]{1,0:T(8,128)(2,1)}, bf16[192,2240]{1,0:T(8,128)(2,1)}, u32[]{:S(2)}, u32[]{:S(2)}) collective-permute-start(bf16[192,2240]{1,0:T(8,128)(2,1)} %get-tuple-element.187), channel_id=1, source_target_pairs={{0,8},{8,16},{16,24},{24,28},{28,20},{20,12},{12,4},{4,0},{1,9},{9... | collective-permute-start | bytes 2580488 | tf_op jit(solution)/shard_map/ppermute | solution.py:181
  475.0 68.6 %collective-permute-start.101 = (bf16[192,2240]{1,0:T(8,128)(2,1)}, bf16[192,2240]{1,0:T(8,128)(2,1)}, u32[]{:S(2)}, u32[]{:S(2)}) collective-permute-start(bf16[192,2240]{1,0:T(8,128)(2,1)} %get-tuple-element.188), channel_id=1, source_target_pairs={{0,4},{8,0},{16,8},{24,16},{28,24},{20,28},{12,20},{4,12},{1,5},{9... | collective-permute-start | bytes 2580488 | tf_op jit(solution)/shard_map/ppermute | solution.py:182
  538.3 42.7 %collective-permute-start.82 = (bf16[192,2240]{1,0:T(8,128)(2,1)}, bf16[192,2240]{1,0:T(8,128)(2,1)S(1)}, u32[]{:S(2)}, u32[]{:S(2)}) collective-permute-start(bf16[192,2240]{1,0:T(8,128)(2,1)} %pad_maximum_fusion.9), channel_id=1, source_target_pairs={{0,8},{8,16},{16,24},{24,28},{28,20},{20,12},{12,4},{4,0},{1,9},{9... | collective-permute-start | bytes 2580488 | tf_op jit(solution)/shard_map/ppermute | solution.py:181
  538.8 42.5 %collective-permute-start.83 = (bf16[192,2240]{1,0:T(8,128)(2,1)}, bf16[192,2240]{1,0:T(8,128)(2,1)S(1)}, u32[]{:S(2)}, u32[]{:S(2)}) collective-permute-start(bf16[192,2240]{1,0:T(8,128)(2,1)} %pad_maximum_fusion.10), channel_id=1, source_target_pairs={{0,4},{8,0},{16,8},{24,16},{28,24},{20,28},{12,20},{4,12},{1,5},{9... | collective-permute-start | bytes 2580488 | tf_op jit(solution)/shard_map/ppermute | solution.py:182
  546.8 65.4 %collective-permute-start.86 = (bf16[192,2240]{1,0:T(8,128)(2,1)}, bf16[192,2240]{1,0:T(8,128)(2,1)}, u32[]{:S(2)}, u32[]{:S(2)}) collective-permute-start(bf16[192,2240]{1,0:T(8,128)(2,1)} %get-tuple-element.197), channel_id=1, source_target_pairs={{0,8},{8,16},{16,24},{24,28},{28,20},{20,12},{12,4},{4,0},{1,9},{9... | collective-permute-start | bytes 2580488 | tf_op jit(solution)/shard_map/ppermute | solution.py:181
  562.9 45.4 %collective-permute-start.78 = (bf16[256,1536]{1,0:T(8,128)(2,1)}, bf16[256,1536]{1,0:T(8,128)(2,1)}, u32[]{:S(2)}, u32[]{:S(2)}) collective-permute-start(bf16[256,1536]{1,0:T(8,128)(2,1)} %get-tuple-element.204), channel_id=1, source_target_pairs={{0,1},{1,0},{2,3},{3,2},{4,5},{5,4},{6,7},{7,6},{8,9},{9,8},{10,11... | collective-permute-start | bytes 2359304 | tf_op jit(solution)/shard_map/ppermute | solution.py:66
  577.5 35.1 %collective-permute-start.87 = (bf16[192,2240]{1,0:T(8,128)(2,1)}, bf16[192,2240]{1,0:T(8,128)(2,1)}, u32[]{:S(2)}, u32[]{:S(2)}) collective-permute-start(bf16[192,2240]{1,0:T(8,128)(2,1)} %get-tuple-element.198), channel_id=1, source_target_pairs={{0,4},{8,0},{16,8},{24,16},{28,24},{20,28},{12,20},{4,12},{1,5},{9... | collective-permute-start | bytes 2580488 | tf_op jit(solution)/shard_map/ppermute | solution.py:182
  581.1 24.6 %collective-permute-start.80 = (bf16[96,1024]{1,0:T(8,128)(2,1)}, bf16[96,1024]{1,0:T(8,128)(2,1)}, u32[]{:S(2)}, u32[]{:S(2)}) collective-permute-start(bf16[96,1024]{1,0:T(8,128)(2,1)} %get-tuple-element.201), channel_id=1, source_target_pairs={{0,8},{8,16},{16,24},{24,28},{28,20},{20,12},{12,4},{4,0},{1,9},{9... | collective-permute-start | bytes 589832 | tf_op jit(solution)/shard_map/ppermute | solution.py:181
  605.6 37.7 %collective-permute-start.77 = (bf16[256,1536]{1,0:T(8,128)(2,1)}, bf16[256,1536]{1,0:T(8,128)(2,1)S(1)}, u32[]{:S(2)}, u32[]{:S(2)}) collective-permute-start(bf16[256,1536]{1,0:T(8,128)(2,1)} %get-tuple-element.205), channel_id=1, source_target_pairs={{0,1},{1,0},{2,3},{3,2},{4,5},{5,4},{6,7},{7,6},{8,9},{9,8},{10,11... | collective-permute-start | bytes 2359304 | tf_op jit(solution)/shard_map/ppermute | solution.py:66
  609.9 35.0 %collective-permute-start.79 = (bf16[256,1536]{1,0:T(8,128)(2,1)S(1)}, bf16[256,1536]{1,0:T(8,128)(2,1)S(1)}, u32[]{:S(2)}, u32[]{:S(2)}) collective-permute-start(bf16[256,1536]{1,0:T(8,128)(2,1)S(1)} %add_convert_fusion), channel_id=1, source_target_pairs={{0,2},{1,3},{2,0},{3,1},{4,6},{5,7},{6,4},{7,5},{8,10},{9,11},{10,... | collective-permute-start | bytes 2359304 | tf_op jit(solution)/shard_map/ppermute | solution.py:66
  611.7 62.9 %collective-permute-start.90 = (bf16[192,2240]{1,0:T(8,128)(2,1)S(1)}, bf16[192,2240]{1,0:T(8,128)(2,1)S(1)}, u32[]{:S(2)}, u32[]{:S(2)}) collective-permute-start(bf16[192,2240]{1,0:T(8,128)(2,1)S(1)} %copy-done.57), channel_id=1, source_target_pairs={{0,8},{8,16},{16,24},{24,28},{28,20},{20,12},{12,4},{4,0},{1,9},{9... | collective-permute-start | bytes 2580488 | tf_op jit(solution)/shard_map/ppermute | solution.py:181
  612.3 28.7 %collective-permute-start.84 = (bf16[192,1024]{1,0:T(8,128)(2,1)S(1)}, bf16[192,1024]{1,0:T(8,128)(2,1)S(1)}, u32[]{:S(2)}, u32[]{:S(2)}) collective-permute-start(bf16[192,1024]{1,0:T(8,128)(2,1)S(1)} %pad_maximum_fusion.15), channel_id=1, source_target_pairs={{0,8},{8,16},{16,24},{24,28},{28,20},{20,12},{12,4},{4,0},{1,9},{9... | collective-permute-start | bytes 1179656 | tf_op jit(solution)/shard_map/ppermute | solution.py:181
  612.6 30.1 %collective-permute-start.85 = (bf16[192,1024]{1,0:T(8,128)(2,1)S(1)}, bf16[192,1024]{1,0:T(8,128)(2,1)S(1)}, u32[]{:S(2)}, u32[]{:S(2)}) collective-permute-start(bf16[192,1024]{1,0:T(8,128)(2,1)S(1)} %pad_maximum_fusion.16), channel_id=1, source_target_pairs={{0,4},{8,0},{16,8},{24,16},{28,24},{20,28},{12,20},{4,12},{1,5},{9... | collective-permute-start | bytes 1179656 | tf_op jit(solution)/shard_map/ppermute | solution.py:182
  640.9 33.6 %collective-permute-start.91 = (bf16[192,2240]{1,0:T(8,128)(2,1)S(1)}, bf16[192,2240]{1,0:T(8,128)(2,1)S(1)}, u32[]{:S(2)}, u32[]{:S(2)}) collective-permute-start(bf16[192,2240]{1,0:T(8,128)(2,1)S(1)} %copy-done.56), channel_id=1, source_target_pairs={{0,4},{8,0},{16,8},{24,16},{28,24},{20,28},{12,20},{4,12},{1,5},{9... | collective-permute-start | bytes 2580488 | tf_op jit(solution)/shard_map/ppermute | solution.py:182
  642.7 61.1 %collective-permute-start.96 = (bf16[192,2240]{1,0:T(8,128)(2,1)S(1)}, bf16[192,2240]{1,0:T(8,128)(2,1)S(1)}, u32[]{:S(2)}, u32[]{:S(2)}) collective-permute-start(bf16[192,2240]{1,0:T(8,128)(2,1)S(1)} %get-tuple-element.211), channel_id=1, source_target_pairs={{0,8},{8,16},{16,24},{24,28},{28,20},{20,12},{12,4},{4,0},{1,9},{9... | collective-permute-start | bytes 2580488 | tf_op jit(solution)/shard_map/ppermute | solution.py:181
  643.3 29.2 %collective-permute-start.88 = (bf16[192,1024]{1,0:T(8,128)(2,1)S(1)}, bf16[192,1024]{1,0:T(8,128)(2,1)S(1)}, u32[]{:S(2)}, u32[]{:S(2)}) collective-permute-start(bf16[192,1024]{1,0:T(8,128)(2,1)S(1)} %get-tuple-element.213), channel_id=1, source_target_pairs={{0,8},{8,16},{16,24},{24,28},{28,20},{20,12},{12,4},{4,0},{1,9},{9... | collective-permute-start | bytes 1179656 | tf_op jit(solution)/shard_map/ppermute | solution.py:181
  644.9 29.4 %collective-permute-start.89 = (bf16[192,1024]{1,0:T(8,128)(2,1)S(1)}, bf16[192,1024]{1,0:T(8,128)(2,1)S(1)}, u32[]{:S(2)}, u32[]{:S(2)}) collective-permute-start(bf16[192,1024]{1,0:T(8,128)(2,1)S(1)} %get-tuple-element.214), channel_id=1, source_target_pairs={{0,4},{8,0},{16,8},{24,16},{28,24},{20,28},{12,20},{4,12},{1,5},{9... | collective-permute-start | bytes 1179656 | tf_op jit(solution)/shard_map/ppermute | solution.py:182
  672.5 31.3 %collective-permute-start.97 = (bf16[192,2240]{1,0:T(8,128)(2,1)S(1)}, bf16[192,2240]{1,0:T(8,128)(2,1)S(1)}, u32[]{:S(2)}, u32[]{:S(2)}) collective-permute-start(bf16[192,2240]{1,0:T(8,128)(2,1)S(1)} %get-tuple-element.212), channel_id=1, source_target_pairs={{0,4},{8,0},{16,8},{24,16},{28,24},{20,28},{12,20},{4,12},{1,5},{9... | collective-permute-start | bytes 2580488 | tf_op jit(solution)/shard_map/ppermute | solution.py:182
  677.0 26.5 %collective-permute-start.93 = (bf16[192,1024]{1,0:T(8,128)(2,1)S(1)}, bf16[192,1024]{1,0:T(8,128)(2,1)S(1)}, u32[]{:S(2)}, u32[]{:S(2)}) collective-permute-start(bf16[192,1024]{1,0:T(8,128)(2,1)S(1)} %get-tuple-element.218), channel_id=1, source_target_pairs={{0,4},{8,0},{16,8},{24,16},{28,24},{20,28},{12,20},{4,12},{1,5},{9... | collective-permute-start | bytes 1179656 | tf_op jit(solution)/shard_map/ppermute | solution.py:182
  681.9 30.2 %collective-permute-start.98 = (bf16[192,2240]{1,0:T(8,128)(2,1)S(1)}, bf16[192,2240]{1,0:T(8,128)(2,1)S(1)}, u32[]{:S(2)}, u32[]{:S(2)}) collective-permute-start(bf16[192,2240]{1,0:T(8,128)(2,1)S(1)} %get-tuple-element.215), channel_id=1, source_target_pairs={{0,8},{8,16},{16,24},{24,28},{28,20},{20,12},{12,4},{4,0},{1,9},{9... | collective-permute-start | bytes 2580488 | tf_op jit(solution)/shard_map/ppermute | solution.py:181
  688.7 31.5 %collective-permute-start.99 = (bf16[192,2240]{1,0:T(8,128)(2,1)S(1)}, bf16[192,2240]{1,0:T(8,128)(2,1)S(1)}, u32[]{:S(2)}, u32[]{:S(2)}) collective-permute-start(bf16[192,2240]{1,0:T(8,128)(2,1)S(1)} %get-tuple-element.216), channel_id=1, source_target_pairs={{0,4},{8,0},{16,8},{24,16},{28,24},{20,28},{12,20},{4,12},{1,5},{9... | collective-permute-start | bytes 2580488 | tf_op jit(solution)/shard_map/ppermute | solution.py:182
  (158 other events, 1876.7 us)
